TPU v7x, 32 devices: a whole 2x2x4 slice. The times are simulated.
32 devices in a mesh: atoms: 16 (over z, x, core), grid: 2 (over y).
Axes of the slice: x: 2, y: 2, z: 4, core: 2. Of those that a mesh axis runs over, the one named last changes fastest.
Arguments:
- basis_values: bfloat16 [16, 2, 2048, 1152], P('atoms', 'grid'), may hold values from -6 to 6
- potential: float32 [16, 2, 2048], P('atoms', 'grid'), may hold values from -6 to 6
- block_lists: int32 [16, 2, 6], P('atoms', 'grid'), may hold values from -1 to 8, as said below
Outputs:
- density_columns: float32 [16, 2, 768, 128], P('atoms', 'grid')
Inputs may be any that keep to these rules, and one draw needn't show every extreme that they name: `block_lists`: entry 0 of every cell's list is 4, the cell itself. For some m from 4 to 6, entries 1 to m - 1 are distinct codes other than 4 whose neighbour cell lies on the line (line positions 0 to 1), and entries from m on are -1. Some cell has m = 6.
All inputs are finite; a program needn't handle non-finite values.
Results may differ from a plain program's by a relative error of at most 0.0017.
Values sent between devices are 32-bit elements; how exact they have to be, the bound alone decides.
No kernel may reach another device: no remote copies, remote signals or barrier semaphores. Data moves between devices by JAX's collectives and lax.ppermute only.
A program may use at most 64 MiB of HBM per device.

v0:
```python
import functools

import jax
import jax.numpy as jnp
from jax import lax
from jax.experimental import pallas as pl
from jax.experimental.pallas import tpu as pltpu
from jax.sharding import PartitionSpec as P

F32 = jnp.float32
BF16 = jnp.bfloat16
REACH = 3


def ring(peers, wrap):
    up = [(i, (i + 1) % peers) for i in range(peers if wrap else peers - 1)]
    return up, [(j, i) for i, j in up]


def extended_2(shard, sides, width, wrap):
    for axis, dim in sides:
        peers, length = (lax.axis_size(axis), shard.shape[dim])
        up, down = ring(peers, wrap)
        last = lax.slice_in_dim(shard, length - width, length, axis=dim)
        first = lax.slice_in_dim(shard, 0, width, axis=dim)
        before = lax.ppermute(last, axis, up)
        after = lax.ppermute(first, axis, down)
        shard = jnp.concatenate([before, shard, after], axis=dim)
    return shard


def combine_three(below_part, centre_part, above_part, dim_index):

    def place(portion, before):
        widths = [(0, 0)] * portion.ndim
        widths[dim_index] = (before, 2 - before)
        return jnp.pad(portion, widths)

    return place(below_part, 0) + place(centre_part, 1) + place(above_part, 2)


def product_kernel(groups, lines, start_ref, values_ref, potential_ref, *refs):
    outs, (held, sems) = refs[:-2], refs[-2:]
    wide = held.shape[2]
    block = wide // lines
    start = start_ref[0]
    copies = []
    for a in range(REACH):
        columns = pl.ds(pl.multiple_of(a * REACH * block + start * block, block), wide)
        copy = pltpu.make_async_copy(values_ref.at[0, 0, :, columns], held.at[a], sems.at[a])
        copy.start()
        copies.append(copy)
    for copy in copies:
        copy.wait()
    level = potential_ref[0, :, :]
    for out, (row, columns) in zip(outs, groups):
        left = held[row].T
        left = (left.astype(F32) * level).astype(BF16)
        for i, column in enumerate(columns):
            out[:, i * wide : (i + 1) * wide] = jnp.dot(
                left, held[column], preferred_element_type=F32
            )


def local_products(values, potential, start, groups, lines):
    points, width = values.shape[2:]
    wide = width // (REACH * REACH) * lines
    flops = sum(2 * points * wide * wide * len(columns) for _, columns in groups)
    return pl.pallas_call(
        functools.partial(product_kernel, groups, lines),
        out_shape=[jax.ShapeDtypeStruct((wide, wide * len(c)), F32) for _, c in groups],
        in_specs=[
            pl.BlockSpec(memory_space=pltpu.SMEM),
            pl.BlockSpec(memory_space=pl.ANY),
            pl.BlockSpec(memory_space=pltpu.VMEM),
        ],
        out_specs=[pl.BlockSpec(memory_space=pltpu.VMEM) for _ in groups],
        scratch_shapes=[
            pltpu.VMEM((REACH, points, wide), BF16),
            pltpu.SemaphoreType.DMA((REACH,)),
        ],
        cost_estimate=pl.CostEstimate(
            flops=flops, bytes_accessed=2 * points * wide * REACH, transcendentals=0
        ),
        name="products",
    )(start, values, potential)


def sign_kernel(slots, block, place, meta_ref, *refs):
    pieces, (out_ref, sh, xf, xb, sb) = refs[:-5], refs[-5:]
    size = sh.shape[0]
    live_count = (meta_ref[0] * block).astype(F32)
    own = meta_ref[1]
    used = [meta_ref[2 + k].astype(F32) for k in range(slots)]
    eye = (
        lax.broadcasted_iota(jnp.int32, (block, block), 0)
        == lax.broadcasted_iota(jnp.int32, (block, block), 1)
    ).astype(F32)

    def read(k, l):
        total = None
        for piece, row, column in place(k, l):
            part = pieces[piece][
                row * block : (row + 1) * block, column * block : (column + 1) * block
            ]
            total = part if total is None else total + part
        return total

    trace = sum(jnp.sum(read(k, k) * eye) * used[k] for k in range(slots))
    mean_level = trace / live_count
    square_sum = jnp.zeros((block, block), F32)
    for k in range(slots):
        for l in range(slots):
            part = read(k, l)
            part = (mean_level * eye - part if k == l else -part) * (used[k] * used[l])
            square_sum = square_sum + part * part
            rows, columns = pl.ds(k * block, block), pl.ds(l * block, block)
            sh[rows, columns] = part
            xb[rows, columns] = part.astype(BF16)
    norm = lax.rsqrt(jnp.full((1, 1), jnp.sum(square_sum) + 1e-06, F32)) * jnp.sqrt(
        jnp.full((1, 1), live_count, F32)
    )
    dot = functools.partial(jnp.dot, preferred_element_type=F32)
    sb[...] = (dot(xb[...], xb[...]) * (norm * norm)).astype(BF16)
    fourth = dot(sb[...], sb[...])
    rho = jnp.sqrt(jnp.sqrt(jnp.sqrt(jnp.full((1, 1), jnp.sum(fourth * fourth) + 1e-06, F32))))
    inverse = 1.0 / rho
    first = norm * inverse
    xf[...] = (1.5 * first) * sh[...] - (0.5 * first * inverse * inverse) * dot(xb[...], sb[...])
    xb[...] = xf[...].astype(BF16)
    sb[...] = dot(xb[...], xb[...]).astype(BF16)
    xf[...] = 1.5 * xf[...] - 0.5 * dot(xb[...], sb[...])
    xb[...] = xf[...].astype(BF16)

    columns = xf[:, pl.ds(pl.multiple_of(own * block, block), block)]

    def thin(v):
        high = v.astype(BF16)
        low = (v - high.astype(F32)).astype(BF16)
        both = dot(xb[...], jnp.concatenate([high, low], axis=1))
        return both[:, :block] + both[:, block:]

    sh[:, :block] = 1.5 * columns - 0.5 * thin(thin(columns))
    for s in range(slots):
        source = meta_ref[2 + slots + s]
        rows = sh[pl.ds(pl.multiple_of(jnp.maximum(source, 0) * block, block), block), :block]
        rows = jnp.where(source >= 0, rows, 0.0)
        out_ref[s * block : (s + 1) * block, :] = 0.5 * (rows + eye if s == 0 else rows)


def sign_columns(meta, pieces, place, slots, block):
    size = slots * block
    vmem = pl.BlockSpec(memory_space=pltpu.VMEM)
    return pl.pallas_call(
        functools.partial(sign_kernel, slots, block, place),
        out_shape=jax.ShapeDtypeStruct((size, block), F32),
        in_specs=[pl.BlockSpec(memory_space=pltpu.SMEM)] + [vmem] * len(pieces),
        out_specs=vmem,
        scratch_shapes=[
            pltpu.VMEM((size, size), F32),
            pltpu.VMEM((size, size), F32),
            pltpu.VMEM((size, size), BF16),
            pltpu.VMEM((size, size), BF16),
        ],
        cost_estimate=pl.CostEstimate(
            flops=12 * size**3, bytes_accessed=4 * size * size, transcendentals=0
        ),
        name="sign",
    )(meta, *pieces)


def shards_dense_line(basis_values, potential, block_lists):
    codes = block_lists[0, 0]
    lines = lax.axis_size("grid")
    position = lax.axis_index("grid")
    width = basis_values.shape[3]
    block = width // (REACH * REACH)
    wide = lines * block
    slots = REACH * lines
    up, down = ring(lax.axis_size("atoms"), True)
    line_shifts = [[(i, (i + s) % lines) for i in range(lines)] for s in range(1, lines)]
    start = (1 - position).astype(jnp.int32)[None]

    def line_sum(part):
        return part + sum(lax.ppermute(part, "grid", shift) for shift in line_shifts)

    low, high = local_products(
        basis_values, potential, start, ((0, (0, 1, 2)), (2, (0, 1, 2))), lines
    )
    from_low = lax.ppermute(high[:, wide:], "atoms", up)
    from_high = lax.ppermute(low[:, : 2 * wide], "atoms", down)
    corners = line_sum(jnp.concatenate([low[:, 2 * wide :], high[:, :wide]], axis=0))
    (middle,) = local_products(basis_values, potential, start, ((1, (0, 1, 2)),), lines)
    own = (
        middle
        + jnp.pad(from_low, ((0, 0), (0, wide)))
        + jnp.pad(from_high, ((0, 0), (wide, 0)))
    )
    own = line_sum(own)
    below = lax.ppermute(own[:, wide:], "atoms", up)
    above = lax.ppermute(own[:, : 2 * wide], "atoms", down)

    def place(k, l):
        a, row = divmod(k, lines)
        b, column = divmod(l, lines)
        if a == 1:
            return [(0, row, b * lines + column)]
        if a == 0:
            return [(1, row, b * lines + column)] if b < 2 else [(3, row, column)]
        return [(2, row, (b - 1) * lines + column)] if b > 0 else [(3, lines + row, column)]

    live = jnp.sum((codes >= 0).astype(jnp.int32))
    source = (codes // REACH) * lines + codes % REACH - 1 + position
    source = jnp.where(codes >= 0, source, -1).astype(jnp.int32)
    blocks = jnp.arange(slots, dtype=jnp.int32)
    used = jnp.sum((source[None, :] == blocks[:, None]).astype(jnp.int32), axis=1)
    meta = jnp.concatenate([live[None], (lines + position)[None].astype(jnp.int32), used, source])
    return sign_columns(meta, (own, below, above, corners), place, slots, block)[None, None]


def shards(basis_values, potential, block_lists):
    values = basis_values[0, 0]
    potential_cell = potential[0, 0]
    slot_codes = block_lists[0, 0]
    slots = slot_codes.shape[0]
    block_size = values.shape[1] // 9
    weighted = (values.astype(jnp.float32) * potential_cell[:, None]).astype(jnp.bfloat16)
    partial_sums = lax.dot_general(
        weighted, values, (((0,), (0,)), ((), ())), preferred_element_type=jnp.float32
    )
    partial_tiles = partial_sums.reshape(3, 3, block_size, 3, 3, block_size)
    extended = extended_2(partial_tiles, (("atoms", 0),), 1, True)
    middle = combine_three(extended[0], extended[2], extended[4], 2)
    extended_line = extended_2(middle, (("grid", 0),), 1, False)
    own_rows = combine_three(extended_line[0], extended_line[2], extended_line[4], 2)
    packed = jnp.stack([own_rows[:, 0:3], own_rows[:, 2:5]])
    arrived = extended_2(packed, (("atoms", 0),), 1, True)
    nearby = jnp.stack([arrived[0], own_rows[:, 1:4], arrived[3]])
    packed_line = jnp.stack([nearby[:, :, :, 0:3], nearby[:, :, :, 2:5]])
    arrived_line = extended_2(packed_line, (("grid", 0),), 1, False)
    gathered = jnp.stack([arrived_line[0], nearby[:, :, :, 1:4], arrived_line[3]], axis=1)
    block_grid = gathered.reshape(9, block_size, 9, block_size)
    selector = (slot_codes[:, None] == jnp.arange(9, dtype=jnp.int32)[None, :]).astype(jnp.float32)
    picked_rows = jnp.einsum("sk,kimj->simj", selector, block_grid, precision=lax.Precision.HIGHEST)
    submatrix = jnp.einsum("simj,tm->sitj", picked_rows, selector, precision=lax.Precision.HIGHEST)
    submatrix = submatrix.reshape(slots * block_size, slots * block_size)
    used = (slot_codes >= 0).astype(jnp.int32)
    source = jnp.where(slot_codes >= 0, jnp.arange(slots, dtype=jnp.int32), -1)
    meta = jnp.concatenate([jnp.sum(used)[None], jnp.zeros((1,), jnp.int32), used, source])
    return sign_columns(
        meta, (submatrix,), lambda k, l: [(0, k, l)], slots, block_size
    )[None, None]


def solution(mesh):
    placed = (P("atoms", "grid", None, None), P("atoms", "grid", None), P("atoms", "grid", None))
    dense = mesh.shape["grid"] == 2 and mesh.shape["atoms"] >= 5

    def body(basis_values, potential, block_lists):
        slots = block_lists.shape[2]
        if dense and slots == REACH * mesh.shape["grid"]:
            return shards_dense_line(basis_values, potential, block_lists)
        return shards(basis_values, potential, block_lists)

    return jax.shard_map(
        body,
        mesh=mesh,
        in_specs=placed,
        out_specs=P("atoms", "grid", None, None),
        check_vma=False,
    )
```

profile of v0, /device:TPU:1, one launch (start us, length us, event | category | flops | bytes accessed | tf_op | source)
XLA Modules:
  0.0 67.7 jit_solution(5044168778436754843)
XLA Ops:
  0.0 5.3 %products.3 = (f32[256,768]{1,0:T(8,128)}, f32[256,768]{1,0:T(8,128)}) custom-call(s32[1]{0:T(128)} %bitcast.6.start_ref, bf16[1,1,2048,1152]{3,2,1,0:T(8,128)(2,1)} %values_ref.3, f32[1,1,2048]{2,1,0:T(1,128)} %potential_ref.3), custom_call_target="tpu_custom_call" | custom-call | flops 1610612736 | bytes 3145728 | tf_op jit(solution)/shard_map/products/pallas_call | solution.py:69
  5.3 1.1 %slice.19 = f32[256,512]{1,0:T(8,128)S(1)} slice(f32[256,768]{1,0:T(8,128)} %get-tuple-element.8), slice={[0:256], [0:512]} | slice | bytes 1048576 | tf_op jit(solution)/shard_map/slice | solution.py:191
  6.4 0.1 collective-permute-start.1
  6.5 1.1 %slice.18 = f32[256,512]{1,0:T(8,128)S(1)} slice(f32[256,768]{1,0:T(8,128)} %get-tuple-element.7), slice={[0:256], [256:768]} | slice | bytes 1048576 | tf_op jit(solution)/shard_map/slice | solution.py:190
  7.6 2.6 %collective-permute-start = (f32[256,512]{1,0:T(8,128)S(1)}, f32[256,512]{1,0:T(8,128)S(1)}, u32[]{:S(2)}, u32[]{:S(2)}) collective-permute-start(f32[256,512]{1,0:T(8,128)S(1)} %slice.18), channel_id=1, source_target_pairs={{0,2},{2,4},{4,6},{6,8},{8,10},{10,12},{12,14},{14,16},{16,18},{18... | collective-permute-start | bytes 1572872 | tf_op jit(solution)/shard_map/ppermute | solution.py:190
  10.2 4.5 %products.2 = f32[256,768]{1,0:T(8,128)} custom-call(s32[1]{0:T(128)} %bitcast.6.start_ref, bf16[1,1,2048,1152]{3,2,1,0:T(8,128)(2,1)} %values_ref.3, f32[1,1,2048]{2,1,0:T(1,128)} %potential_ref.3), custom_call_target="tpu_custom_call" | custom-call | flops 805306368 | bytes 3145728 | tf_op jit(solution)/shard_map/products/pallas_call | solution.py:69
  14.8 0.0 copy-start.1
  14.8 1.2 %collective-permute-done.1 = f32[256,512]{1,0:T(8,128)S(1)} collective-permute-done((f32[256,512]{1,0:T(8,128)S(1)}, f32[256,512]{1,0:T(8,128)S(1)}, u32[]{:S(2)}, u32[]{:S(2)}) %collective-permute-start.1) | collective-permute-done | bytes 524320 | tf_op jit(solution)/shard_map/ppermute | solution.py:191
  15.9 5.8 %collective-permute-done = f32[256,512]{1,0:T(8,128)S(1)} collective-permute-done((f32[256,512]{1,0:T(8,128)S(1)}, f32[256,512]{1,0:T(8,128)S(1)}, u32[]{:S(2)}, u32[]{:S(2)}) %collective-permute-start) | collective-permute-done | bytes 524320 | tf_op jit(solution)/shard_map/ppermute | solution.py:190
  21.7 1.2 %pad_add_fusion = f32[256,768]{1,0:T(8,128)S(1)} fusion(f32[256,512]{1,0:T(8,128)S(1)} %collective-permute-done.1, f32[256,768]{1,0:T(8,128)} %products.2, f32[256,512]{1,0:T(8,128)S(1)} %collective-permute-done), kind=kLoop, calls=%fused_computation | loop fusion | flops 393216 | bytes 2621440 | tf_op jit(solution)/shard_map/add | solution.py:195
  23.0 1.3 %collective-permute-start.2 = (f32[256,768]{1,0:T(8,128)S(1)}, f32[256,768]{1,0:T(8,128)S(1)}, u32[]{:S(2)}, u32[]{:S(2)}) collective-permute-start(f32[256,768]{1,0:T(8,128)S(1)} %pad_add_fusion), channel_id=1, source_target_pairs={{0,1},{1,0},{2,3},{3,2},{4,5},{5,4},{6,7},{7,6},{8,9},{9,8},{10,11... | collective-permute-start | bytes 2359304 | tf_op jit(solution)/shard_map/ppermute | solution.py:185
  24.3 1.0 %slice.23 = f32[256,256]{1,0:T(8,128)S(1)} slice(f32[256,768]{1,0:T(8,128)} %get-tuple-element.7), slice={[0:256], [0:256]} | slice | bytes 524288 | tf_op jit(solution)/shard_map/slice | solution.py:192
  25.2 1.0 %slice.22 = f32[256,256]{1,0:T(8,128)S(1)} slice(f32[256,768]{1,0:T(8,128)} %get-tuple-element.8), slice={[0:256], [512:768]} | slice | bytes 524288 | tf_op jit(solution)/shard_map/slice | solution.py:192
  26.2 0.3 collective-permute-start.5
  26.5 12.9 %collective-permute-done.2 = f32[256,768]{1,0:T(8,128)S(1)} collective-permute-done((f32[256,768]{1,0:T(8,128)S(1)}, f32[256,768]{1,0:T(8,128)S(1)}, u32[]{:S(2)}, u32[]{:S(2)}) %collective-permute-start.2) | collective-permute-done | bytes 786464 | tf_op jit(solution)/shard_map/ppermute | solution.py:185
  39.5 0.1 add.63.refs_0_
  39.5 0.0 copy-start
  39.6 0.1 fusion.4
  39.7 6.7 %collective-permute-start.4 = (f32[256,512]{1,0:T(8,128)S(1)}, f32[256,512]{1,0:T(8,128)}, u32[]{:S(2)}, u32[]{:S(2)}) collective-permute-start(f32[256,512]{1,0:T(8,128)S(1)} %get-tuple-element.9), channel_id=1, source_target_pairs={{2,0},{4,2},{6,4},{8,6},{10,8},{12,10},{14,12},{16,14},{18,16},{20... | collective-permute-start | bytes 1572872 | tf_op jit(solution)/shard_map/ppermute | solution.py:201
  46.4 0.0 collective-permute-start.3
  46.4 0.0 copy-done.1
  46.4 0.6 fusion.2
  47.0 0.1 convert_reduce_fusion
  47.1 1.3 %pad_add_fusion.1.meta_ref = s32[14]{0:T(128)} fusion(s32[6]{0:T(128)S(1)} %get-tuple-element.12, s32[6]{0:T(128)S(1)} %convert_reduce_fusion, s32[1]{0:T(128)} %bitcast.2, s32[1]{0:T(128)} %bitcast.1), kind=kLoop, calls=%fused_computation.11 | loop fusion | flops 42 | bytes 112 | tf_op jit(solution)/shard_map/concatenate | solution.py:217
  48.4 2.3 %collective-permute-done.5 = f32[512,256]{1,0:T(8,128)S(1)} collective-permute-done((f32[512,256]{1,0:T(8,128)S(1)}, f32[512,256]{1,0:T(8,128)S(1)}, u32[]{:S(2)}, u32[]{:S(2)}) %collective-permute-start.5) | collective-permute-done | bytes 524320 | tf_op jit(solution)/shard_map/ppermute | solution.py:185
  50.7 0.9 %fusion.3.refs_3_ = f32[512,256]{1,0:T(8,128)} fusion(f32[512,256]{1,0:T(8,128)S(1)} %collective-permute-done.5, f32[256,256]{1,0:T(8,128)S(1)} %slice.23, f32[256,256]{1,0:T(8,128)S(1)} %slice.22), kind=kLoop, calls=%fused_computation.12 | loop fusion | flops 262144 | bytes 1572864 | tf_op jit(solution)/shard_map/add | solution.py:185
  51.6 6.5 %collective-permute-done.4.refs_2_ = f32[256,512]{1,0:T(8,128)} collective-permute-done((f32[256,512]{1,0:T(8,128)S(1)}, f32[256,512]{1,0:T(8,128)}, u32[]{:S(2)}, u32[]{:S(2)}) %collective-permute-start.4) | collective-permute-done | bytes 524320 | tf_op jit(solution)/shard_map/ppermute | solution.py:201
  58.1 0.0 collective-permute-done.3.refs_1_
  58.1 0.0 copy-done
  58.1 9.6 %sign.14 = f32[768,128]{1,0:T(8,128)} custom-call(s32[14]{0:T(128)} %pad_add_fusion.1.meta_ref, f32[256,768]{1,0:T(8,128)} %copy-done, f32[256,512]{1,0:T(8,128)} %collective-permute-done.3.refs_1_, f32[256,512]{1,0:T(8,128)} %collective-permute-done.4.refs_2_, f32[512,256]{1,0:T(8,128)} %fusion.3.refs_3_), custom_call_target="tpu_custom_call" | custom-call | flops 5435817984 | bytes 2359296 | tf_op jit(solution)/shard_map/sign/pallas_call | solution.py:154
  (1 shorter events, 0.0 us)
Async XLA Ops:
  6.4 9.5 %collective-permute-start.1 = (f32[256,512]{1,0:T(8,128)S(1)}, f32[256,512]{1,0:T(8,128)S(1)}, u32[]{:S(2)}, u32[]{:S(2)}) collective-permute-start(f32[256,512]{1,0:T(8,128)S(1)} %slice.19), channel_id=1, source_target_pairs={{2,0},{4,2},{6,4},{8,6},{10,8},{12,10},{14,12},{16,14},{18,16},{20... | collective-permute-start | bytes 1572872 | tf_op jit(solution)/shard_map/ppermute | solution.py:191
  7.6 14.1 %collective-permute-start = (f32[256,512]{1,0:T(8,128)S(1)}, f32[256,512]{1,0:T(8,128)S(1)}, u32[]{:S(2)}, u32[]{:S(2)}) collective-permute-start(f32[256,512]{1,0:T(8,128)S(1)} %slice.18), channel_id=1, source_target_pairs={{0,2},{2,4},{4,6},{6,8},{8,10},{10,12},{12,14},{14,16},{16,18},{18... | collective-permute-start | bytes 1572872 | tf_op jit(solution)/shard_map/ppermute | solution.py:190
  14.8 31.6 %copy-start.1 = (s32[1,1,6]{2,1,0:T(1,128)S(1)}, s32[1,1,6]{2,1,0:T(1,128)}, u32[]{:S(2)}) copy-start(s32[1,1,6]{2,1,0:T(1,128)} %param.5) | copy-start | bytes 76
  23.0 16.5 %collective-permute-start.2 = (f32[256,768]{1,0:T(8,128)S(1)}, f32[256,768]{1,0:T(8,128)S(1)}, u32[]{:S(2)}, u32[]{:S(2)}) collective-permute-start(f32[256,768]{1,0:T(8,128)S(1)} %pad_add_fusion), channel_id=1, source_target_pairs={{0,1},{1,0},{2,3},{3,2},{4,5},{5,4},{6,7},{7,6},{8,9},{9,8},{10,11... | collective-permute-start | bytes 2359304 | tf_op jit(solution)/shard_map/ppermute | solution.py:185
  26.2 24.4 %collective-permute-start.5 = (f32[512,256]{1,0:T(8,128)S(1)}, f32[512,256]{1,0:T(8,128)S(1)}, u32[]{:S(2)}, u32[]{:S(2)}) collective-permute-start(f32[512,256]{1,0:T(8,128)S(1)} %pad_maximum_fusion), channel_id=1, source_target_pairs={{0,1},{1,0},{2,3},{3,2},{4,5},{5,4},{6,7},{7,6},{8,9},{9,8},{10,11... | collective-permute-start | bytes 1572872 | tf_op jit(solution)/shard_map/ppermute | solution.py:185
  39.5 18.5 %copy-start = (f32[256,768]{1,0:T(8,128)}, f32[256,768]{1,0:T(8,128)S(1)}, u32[]{:S(2)}) copy-start(f32[256,768]{1,0:T(8,128)S(1)} %add.63.refs_0_) | copy-start | bytes 2359300
  39.7 18.4 %collective-permute-start.4 = (f32[256,512]{1,0:T(8,128)S(1)}, f32[256,512]{1,0:T(8,128)}, u32[]{:S(2)}, u32[]{:S(2)}) collective-permute-start(f32[256,512]{1,0:T(8,128)S(1)} %get-tuple-element.9), channel_id=1, source_target_pairs={{2,0},{4,2},{6,4},{8,6},{10,8},{12,10},{14,12},{16,14},{18,16},{20... | collective-permute-start | bytes 1572872 | tf_op jit(solution)/shard_map/ppermute | solution.py:201
  46.4 11.7 %collective-permute-start.3 = (f32[256,512]{1,0:T(8,128)S(1)}, f32[256,512]{1,0:T(8,128)}, u32[]{:S(2)}, u32[]{:S(2)}) collective-permute-start(f32[256,512]{1,0:T(8,128)S(1)} %get-tuple-element.10), channel_id=1, source_target_pairs={{0,2},{2,4},{4,6},{6,8},{8,10},{10,12},{12,14},{14,16},{16,18},{18... | collective-permute-start | bytes 1572872 | tf_op jit(solution)/shard_map/ppermute | solution.py:200
where the time goes:
time: 68.1 us; the launch traced here: 67.7 us
  waiting for transfers between devices  28.6 us (42%)
  Pallas kernels  19.5 us (29%)
  starting transfers between devices  11 us (16%)
  other arithmetic  4.29 us (6%)
  local copies, waits for them, and re-layouts  4.2 us (6%)
    ppermute x2, waiting for transfers between devices, line_sum(): lax.ppermute(part, 'grid', shift)  15.2 us
    pallas_call x2, Pallas kernels, local_products(): pl.pallas_call(functools.partial(product_kernel, groups, lines), out_shap...  9.87 us
    pallas_call x1, Pallas kernels, sign_columns(): pl.pallas_call(functools.partial(sign_kernel, slots, block, place), out_s...  9.6 us
    ppermute x1, starting transfers between devices, shards_dense_line(): above = lax.ppermute(own[:, :2 * wide], 'atoms', down)  6.68 us
    ppermute x1, waiting for transfers between devices, shards_dense_line(): above = lax.ppermute(own[:, :2 * wide], 'atoms', down)  6.48 us
    ppermute x1, waiting for transfers between devices, shards_dense_line(): from_low = lax.ppermute(high[:, wide:], 'atoms', up)  5.79 us
    ppermute x1, starting transfers between devices, shards_dense_line(): from_low = lax.ppermute(high[:, wide:], 'atoms', up)  2.64 us
    ppermute x2, starting transfers between devices, line_sum(): lax.ppermute(part, 'grid', shift)  1.6 us
  transfers between devices with their start and end apart: 6, of which 5 were waited for; matrix products, arithmetic and copies ran while one was open for 9% of the time, Pallas kernels for 7%

commit v1 on v0

v1 whole, which is shorter than its diff:
```python
import functools

import jax
import jax.numpy as jnp
from jax import lax
from jax.experimental import pallas as pl
from jax.experimental.pallas import tpu as pltpu
from jax.sharding import PartitionSpec as P

F32 = jnp.float32
BF16 = jnp.bfloat16
REACH = 3
KERNEL_BYTES = 32 * 1024 * 1024
LOADING_BYTES = 50 * 1024 * 1024


def ring(peers, wrap):
    up = [(i, (i + 1) % peers) for i in range(peers if wrap else peers - 1)]
    return up, [(j, i) for i, j in up]


def extended_2(shard, sides, width, wrap):
    for axis, dim in sides:
        peers, length = (lax.axis_size(axis), shard.shape[dim])
        up, down = ring(peers, wrap)
        last = lax.slice_in_dim(shard, length - width, length, axis=dim)
        first = lax.slice_in_dim(shard, 0, width, axis=dim)
        before = lax.ppermute(last, axis, up)
        after = lax.ppermute(first, axis, down)
        shard = jnp.concatenate([before, shard, after], axis=dim)
    return shard


def combine_three(below_part, centre_part, above_part, dim_index):

    def place(portion, before):
        widths = [(0, 0)] * portion.ndim
        widths[dim_index] = (before, 2 - before)
        return jnp.pad(portion, widths)

    return place(below_part, 0) + place(centre_part, 1) + place(above_part, 2)


def product_kernel(outputs, lines, chunks, start_ref, values_ref, potential_ref, *refs):
    outs, (held, turned, total, sems) = refs[:-4], refs[-4:]
    depth, size = held.shape[1:]
    wide = size // REACH
    block = wide // lines
    start = start_ref[0]
    copies = []
    for c in range(chunks):
        for a in range(REACH):
            columns = pl.ds(pl.multiple_of(a * REACH * block + start * block, block), wide)
            copies.append(
                pltpu.make_async_copy(
                    values_ref.at[0, 0, pl.ds(c * depth, depth), columns],
                    held.at[c, :, pl.ds(a * wide, wide)],
                    sems.at[c, a],
                )
            )
            copies[-1].start()

    def prepare(c):
        for a in range(REACH):
            copies[c * REACH + a].wait()
        level = potential_ref[0, :, c * depth : (c + 1) * depth]
        turned[c % 2] = (held[c].T.astype(F32) * level).astype(BF16)

    prepare(0)
    for c in range(chunks):
        if c + 1 < chunks:
            prepare(c + 1)
        for a in range(REACH):
            columns = pl.ds(a * wide, wide)
            part = jnp.dot(turned[c % 2], held[c, :, columns], preferred_element_type=F32)
            total[:, columns] = part if c == 0 else total[:, columns] + part

    def mean(i, j):
        rows, columns = pl.ds(i * block, block), pl.ds(j * block, block)
        return 0.5 * (total[rows, columns] + total[columns, rows].T)

    for out, pairs in zip(outs, outputs):
        for n, (i, j) in enumerate(pairs):
            out[n * block : (n + 1) * block, :] = mean(i, j)


def local_products(values, potential, start, outputs, lines):
    points, width = values.shape[2:]
    block = width // (REACH * REACH)
    size = block * lines * REACH
    chunks = 4
    vmem = pl.BlockSpec(memory_space=pltpu.VMEM)
    return pl.pallas_call(
        functools.partial(product_kernel, outputs, lines, chunks),
        out_shape=[jax.ShapeDtypeStruct((len(pairs) * block, block), F32) for pairs in outputs],
        in_specs=[
            pl.BlockSpec(memory_space=pltpu.SMEM),
            pl.BlockSpec(memory_space=pltpu.HBM),
            vmem,
        ],
        out_specs=[vmem] * len(outputs),
        scratch_shapes=[
            pltpu.VMEM((chunks, points // chunks, size), BF16),
            pltpu.VMEM((2, size, points // chunks), BF16),
            pltpu.VMEM((size, size), F32),
            pltpu.SemaphoreType.DMA((chunks, REACH)),
        ],
        compiler_params=pltpu.CompilerParams(vmem_limit_bytes=LOADING_BYTES),
        cost_estimate=pl.CostEstimate(
            flops=2 * points * size * size, bytes_accessed=2 * points * size, transcendentals=0
        ),
        name="products",
    )(start, values, potential)


def sign_kernel(slots, block, own_tile, place, meta_ref, *refs):
    pieces, (out_ref, xf, cf, yf, xb, sb, yb) = refs[:-7], refs[-7:]
    size, tile = yf.shape
    tiles, per_tile = size // tile, tile // block
    live_count = (meta_ref[0] * block).astype(F32)
    used = [meta_ref[2 + k].astype(F32) for k in range(slots)]
    eye = (
        lax.broadcasted_iota(jnp.int32, (block, block), 0)
        == lax.broadcasted_iota(jnp.int32, (block, block), 1)
    ).astype(F32)
    dot = functools.partial(jnp.dot, preferred_element_type=F32)

    def at(i, width=tile):
        return pl.ds(i * width, width)

    def read(k, l):
        total = None
        for piece, n in place(k, l):
            part = pieces[piece][n * block : (n + 1) * block, :]
            total = part if total is None else total + part
        return total

    def fold(x):
        return jnp.sum(x.reshape(x.shape[0] // 8, 8, x.shape[1]), axis=0)

    def columns_of(left, right):
        for j in range(tiles):
            yield j, dot(left[: (j + 1) * tile, :], right[:, at(j)])

    def keep(to, j, upper):
        upper = upper.astype(BF16)
        to[: (j + 1) * tile, at(j)] = upper
        for i in range(j):
            to[at(j), at(i)] = upper[i * tile : (i + 1) * tile].T

    trace = sum(jnp.sum(read(k, k) * eye) * used[k] for k in range(slots))
    mean_level = trace / live_count
    square_sum = jnp.zeros((8, block), F32)
    for k in range(slots):
        for l in range(k, slots):
            part = read(k, l)
            part = (mean_level * eye - part if k == l else -part) * (used[k] * used[l])
            square_sum = square_sum + fold(part * part) * (1.0 if k == l else 2.0)
            rows, columns = at(k, block), at(l, block)
            xf[rows, columns] = part
            xb[rows, columns] = part.astype(BF16)
            if k < l:
                mirror = part.T
                xb[columns, rows] = mirror.astype(BF16)
                if k // per_tile == l // per_tile:
                    xf[columns, rows] = mirror
    norm = lax.rsqrt(jnp.full((1, 1), jnp.sum(square_sum) + 1e-06, F32)) * jnp.sqrt(
        jnp.full((1, 1), live_count, F32)
    )
    for j, square in columns_of(xb, xb):
        keep(sb, j, square * (norm * norm))
    fourth_sum = jnp.zeros((8, tile), F32)
    for j, fourth in columns_of(sb, sb):
        fourth = fourth * fourth
        fourth_sum = fourth_sum + fold(fourth[j * tile :])
        if j:
            fourth_sum = fourth_sum + 2.0 * fold(fourth[: j * tile])
    for j, cube in columns_of(xb, sb):
        cf[: (j + 1) * tile, at(j)] = cube
    rho = jnp.sqrt(jnp.sqrt(jnp.sqrt(jnp.full((1, 1), jnp.sum(fourth_sum) + 1e-06, F32))))
    inverse = 1.0 / rho
    first = norm * inverse
    for j in range(tiles):
        rows, columns = pl.ds(0, (j + 1) * tile), at(j)
        upper = (1.5 * first) * xf[rows, columns] - (0.5 * first * inverse * inverse) * cf[
            rows, columns
        ]
        xf[rows, columns] = upper
        keep(xb, j, upper)
    for j, square in columns_of(xb, xb):
        keep(sb, j, square)
    for j, cube in columns_of(xb, sb):
        upper = 1.5 * xf[: (j + 1) * tile, at(j)] - 0.5 * cube
        keep(yb, j, upper)
        if j == own_tile:
            yf[: (j + 1) * tile, :] = upper
        elif j > own_tile:
            yf[at(j), :] = upper[own_tile * tile : (own_tile + 1) * tile].T

    columns = yf[:, pl.ds(pl.multiple_of(meta_ref[1] * block, block), block)]

    def thin(v):
        high = v.astype(BF16)
        low = (v - high.astype(F32)).astype(BF16)
        both = dot(yb[...], jnp.concatenate([high, low], axis=1))
        return both[:, :block] + both[:, block:]

    xf[:, :block] = 1.5 * columns - 0.5 * thin(thin(columns))
    for s in range(slots):
        source = meta_ref[2 + slots + s]
        rows = xf[pl.ds(pl.multiple_of(jnp.maximum(source, 0) * block, block), block), :block]
        rows = jnp.where(source >= 0, rows, 0.0)
        out_ref[s * block : (s + 1) * block, :] = 0.5 * (rows + eye if s == 0 else rows)


def sign_columns(meta, pieces, place, slots, block, own_tile):
    size = slots * block
    tile = block * (2 if slots % 2 == 0 else 1)
    vmem = pl.BlockSpec(memory_space=pltpu.VMEM)
    return pl.pallas_call(
        functools.partial(sign_kernel, slots, block, own_tile, place),
        out_shape=jax.ShapeDtypeStruct((size, block), F32),
        in_specs=[pl.BlockSpec(memory_space=pltpu.SMEM)] + [vmem] * len(pieces),
        out_specs=vmem,
        scratch_shapes=[
            pltpu.VMEM((size, size), F32),
            pltpu.VMEM((size, size), F32),
            pltpu.VMEM((size, tile), F32),
            pltpu.VMEM((size, size), BF16),
            pltpu.VMEM((size, size), BF16),
            pltpu.VMEM((size, size), BF16),
        ],
        compiler_params=pltpu.CompilerParams(vmem_limit_bytes=KERNEL_BYTES),
        cost_estimate=pl.CostEstimate(
            flops=8 * size**3, bytes_accessed=4 * size * size, transcendentals=0
        ),
        name="sign",
    )(meta, *pieces)


def shards_dense_line(basis_values, potential, block_lists):
    codes = block_lists[0, 0]
    lines = lax.axis_size("grid")
    position = lax.axis_index("grid")
    block = basis_values.shape[3] // (REACH * REACH)
    slots = REACH * lines
    up, down = ring(lax.axis_size("atoms"), True)
    line_shifts = [[(i, (i + s) % lines) for i in range(lines)] for s in range(1, lines)]
    start = (1 - position).astype(jnp.int32)[None]

    def line_parts(part):
        return [lax.ppermute(part, "grid", shift) for shift in line_shifts]

    half = lines // 2
    triangle = [(r, q) for r in range(lines) for q in range(r, lines)]

    def within(a):
        return [(a * lines + r, a * lines + q) for r, q in triangle]

    def across(a, b, rows):
        return [(a * lines + r, b * lines + q) for r in rows for q in range(lines)]

    early, late = range(half), range(half, lines)
    up_own, up_side, down_own, down_side, outer, own, side = local_products(
        basis_values,
        potential,
        start,
        (
            within(2),
            across(1, 2, early),
            within(0),
            across(0, 1, late),
            across(0, 2, range(lines)),
            within(1),
            across(0, 1, early) + across(1, 2, late),
        ),
        lines,
    )
    outer_parts = [outer] + line_parts(outer)
    own = own + lax.ppermute(up_own, "atoms", up) + lax.ppermute(down_own, "atoms", down)
    up_side, down_side = lax.ppermute(up_side, "atoms", up), lax.ppermute(down_side, "atoms", down)
    side = side + jnp.concatenate([up_side, down_side])
    own = sum(line_parts(own), own)
    side = sum(line_parts(side), side)
    below_own = lax.ppermute(own, "atoms", up)
    above_own = lax.ppermute(own, "atoms", down)
    cut = half * lines * block
    below_side = lax.ppermute(side[cut:], "atoms", up)
    above_side = lax.ppermute(side[:cut], "atoms", down)
    pieces = [own, side, below_own, above_own, below_side, above_side] + outer_parts

    def place(k, l):
        (a, r), (b, q) = divmod(k, lines), divmod(l, lines)
        if a == b:
            return [((2, 0, 3)[a], triangle.index((r, q)))]
        if b - a == 2:
            return [(n, r * lines + q) for n in range(6, len(pieces))]
        if r < half:
            return [((1, 5)[a], r * lines + q)]
        if a == 0:
            return [(4, (r - half) * lines + q)]
        return [(1, r * lines + q)]

    live = jnp.sum((codes >= 0).astype(jnp.int32))
    source = (codes // REACH) * lines + codes % REACH - 1 + position
    source = jnp.where(codes >= 0, source, -1).astype(jnp.int32)
    blocks = jnp.arange(slots, dtype=jnp.int32)
    used = jnp.sum((source[None, :] == blocks[:, None]).astype(jnp.int32), axis=1)
    meta = jnp.concatenate([live[None], position[None].astype(jnp.int32), used, source])
    return sign_columns(meta, pieces, place, slots, block, 1)[None, None]


def shards(basis_values, potential, block_lists):
    values = basis_values[0, 0]
    potential_cell = potential[0, 0]
    slot_codes = block_lists[0, 0]
    slots = slot_codes.shape[0]
    block_size = values.shape[1] // 9
    weighted = (values.astype(jnp.float32) * potential_cell[:, None]).astype(jnp.bfloat16)
    partial_sums = lax.dot_general(
        weighted, values, (((0,), (0,)), ((), ())), preferred_element_type=jnp.float32
    )
    partial_sums = 0.5 * (partial_sums + partial_sums.T)
    partial_tiles = partial_sums.reshape(3, 3, block_size, 3, 3, block_size)
    extended = extended_2(partial_tiles, (("atoms", 0),), 1, True)
    middle = combine_three(extended[0], extended[2], extended[4], 2)
    extended_line = extended_2(middle, (("grid", 0),), 1, False)
    own_rows = combine_three(extended_line[0], extended_line[2], extended_line[4], 2)
    packed = jnp.stack([own_rows[:, 0:3], own_rows[:, 2:5]])
    arrived = extended_2(packed, (("atoms", 0),), 1, True)
    nearby = jnp.stack([arrived[0], own_rows[:, 1:4], arrived[3]])
    packed_line = jnp.stack([nearby[:, :, :, 0:3], nearby[:, :, :, 2:5]])
    arrived_line = extended_2(packed_line, (("grid", 0),), 1, False)
    gathered = jnp.stack([arrived_line[0], nearby[:, :, :, 1:4], arrived_line[3]], axis=1)
    block_grid = gathered.reshape(9, block_size, 9, block_size)
    selector = (slot_codes[:, None] == jnp.arange(9, dtype=jnp.int32)[None, :]).astype(jnp.float32)
    picked_rows = jnp.einsum("sk,kimj->simj", selector, block_grid, precision=lax.Precision.HIGHEST)
    submatrix = jnp.einsum("simj,tm->sitj", picked_rows, selector, precision=lax.Precision.HIGHEST)
    pieces = [submatrix[k, :, k:].transpose(1, 0, 2).reshape(-1, block_size) for k in range(slots)]
    used = (slot_codes >= 0).astype(jnp.int32)
    source = jnp.where(slot_codes >= 0, jnp.arange(slots, dtype=jnp.int32), -1)
    meta = jnp.concatenate([jnp.sum(used)[None], jnp.zeros((1,), jnp.int32), used, source])
    return sign_columns(meta, pieces, lambda k, l: [(k, l - k)], slots, block_size, 0)[None, None]


def solution(mesh):
    placed = (P("atoms", "grid", None, None), P("atoms", "grid", None), P("atoms", "grid", None))
    dense = mesh.shape["grid"] == 2 and mesh.shape["atoms"] >= 5

    def body(basis_values, potential, block_lists):
        if dense and block_lists.shape[2] == REACH * mesh.shape["grid"]:
            return shards_dense_line(basis_values, potential, block_lists)
        return shards(basis_values, potential, block_lists)

    return jax.shard_map(
        body,
        mesh=mesh,
        in_specs=placed,
        out_specs=P("atoms", "grid", None, None),
        check_vma=False,
    )
```

time: 68.1 us -> 49.6 us (0.73)
  the two profiles are of different devices: /device:TPU:1 before, /device:TPU:0 now
where the time goes in v1:
time: 49.6 us; the launch traced here: 49.4 us
  starting transfers between devices  20.5 us (41%)
  waiting for transfers between devices  14.4 us (29%)
  Pallas kernels  12.1 us (24%)
  other arithmetic  1.61 us (3%)
  local copies, waits for them, and re-layouts  0.72 us (1%)
    ppermute x3, waiting for transfers between devices, line_parts(): return [lax.ppermute(part, 'grid', shift) for shift in line_shifts]  6.86 us
    pallas_call x1, Pallas kernels, sign_columns(): pl.pallas_call(functools.partial(sign_kernel, slots, block, own_tile, pla...  6.39 us
    pallas_call x1, Pallas kernels, local_products(): pl.pallas_call(functools.partial(product_kernel, outputs, lines, chunks),...  5.74 us
    ppermute x1, starting transfers between devices, shards_dense_line(): lax.ppermute(down_side, 'atoms', down)  5.02 us
    ppermute x1, waiting for transfers between devices, shards_dense_line(): below_own = lax.ppermute(own, 'atoms', up)  4.6 us
    ppermute x1, starting transfers between devices, shards_dense_line(): above_own = lax.ppermute(own, 'atoms', down)  4.44 us
    ppermute x1, starting transfers between devices, shards_dense_line(): lax.ppermute(down_own, 'atoms', down)  4.44 us
    ppermute x3, starting transfers between devices, line_parts(): return [lax.ppermute(part, 'grid', shift) for shift in line_shifts]  4.08 us
  transfers between devices with their start and end apart: 11, of which 6 were waited for; matrix products, arithmetic and copies ran while one was open for 3% of the time, Pallas kernels for 0%

profile of v1, /device:TPU:0, one launch (start us, length us, event | category | flops | bytes accessed | tf_op | source)
XLA Modules:
  0.0 49.4 jit_solution(16073853462598482429)
XLA Ops:
  0.0 0.0 copy-start
  0.0 0.7 %copy-done = f32[1,1,2048]{2,1,0:T(1,128)S(1)} copy-done((f32[1,1,2048]{2,1,0:T(1,128)S(1)}, f32[1,1,2048]{2,1,0:T(1,128)}, u32[]{:S(2)}) %copy-start) | copy-done | bytes 8216
  0.7 0.0 copy-start.1
  0.7 5.7 %products.1 = (f32[384,128]{1,0:T(8,128)S(1)}, f32[256,128]{1,0:T(8,128)S(1)}, f32[384,128]{1,0:T(8,128)S(1)}, f32[256,128]{1,0:T(8,128)S(1)}, f32[512,128]{1,0:...) custom-call(s32[1]{0:T(128)} %bitcast.6.start_ref, bf16[1,1,2048,1152]{3,2,1,0:T(8,128)(2,1)} %values_ref.1, ...), custom_call_target="tpu_custom_call" | custom-call | flops 2415919104 | bytes 3145728 | tf_op jit(solution)/shard_map/products/pallas_call | solution.py:93
  6.4 0.5 %collective-permute-start.3 = (f32[256,128]{1,0:T(8,128)S(1)}, f32[256,128]{1,0:T(8,128)S(1)}, u32[]{:S(2)}, u32[]{:S(2)}) collective-permute-start(f32[256,128]{1,0:T(8,128)S(1)} %get-tuple-element.16), channel_id=1, source_target_pairs={{0,2},{2,4},{4,6},{6,8},{8,10},{10,12},{12,14},{14,16},{16,18},{18... | collective-permute-start | bytes 393224 | tf_op jit(solution)/shard_map/ppermute | solution.py:281
  7.0 5.0 %collective-permute-start.4 = (f32[256,128]{1,0:T(8,128)S(1)}, f32[256,128]{1,0:T(8,128)S(1)}, u32[]{:S(2)}, u32[]{:S(2)}) collective-permute-start(f32[256,128]{1,0:T(8,128)S(1)} %get-tuple-element.17), channel_id=1, source_target_pairs={{2,0},{4,2},{6,4},{8,6},{10,8},{12,10},{14,12},{16,14},{18,16},{20... | collective-permute-start | bytes 393224 | tf_op jit(solution)/shard_map/ppermute | solution.py:281
  12.0 0.0 collective-permute-start
  12.0 4.4 %collective-permute-start.1 = (f32[384,128]{1,0:T(8,128)S(1)}, f32[384,128]{1,0:T(8,128)S(1)}, u32[]{:S(2)}, u32[]{:S(2)}) collective-permute-start(f32[384,128]{1,0:T(8,128)S(1)} %get-tuple-element.14), channel_id=1, source_target_pairs={{2,0},{4,2},{6,4},{8,6},{10,8},{12,10},{14,12},{16,14},{18,16},{20... | collective-permute-start | bytes 589832 | tf_op jit(solution)/shard_map/ppermute | solution.py:280
  16.5 1.9 %collective-permute-start.10 = (f32[512,128]{1,0:T(8,128)S(1)}, f32[512,128]{1,0:T(8,128)S(1)}, u32[]{:S(2)}, u32[]{:S(2)}) collective-permute-start(f32[512,128]{1,0:T(8,128)S(1)} %get-tuple-element.18.refs_6_), channel_id=1, source_target_pairs={{0,1},{1,0},{2,3},{3,2},{4,5},{5,4},{6,7},{7,6},{8,9},{9,8},{10,11... | collective-permute-start | bytes 786440 | tf_op jit(solution)/shard_map/ppermute | solution.py:252
  18.4 0.0 collective-permute-done.3
  18.4 0.0 collective-permute-done.4
  18.4 0.2 collective-permute-start.5
  18.6 0.0 copy-done.1
  18.6 0.7 %fusion.2 = (s32[]{:T(128)}, s32[6]{0:T(128)S(1)}) fusion(s32[1,1,6]{2,1,0:T(1,128)S(1)} %copy-done.1, s32[]{:T(128)} %axis_index.12), kind=kLoop, calls=%fused_computation.10 | loop fusion | flops 119 | bytes 56 | tf_op jit(solution)/shard_map/reduce_sum | solution.py:304
  19.2 0.6 %collective-permute-done = f32[384,128]{1,0:T(8,128)S(1)} collective-permute-done((f32[384,128]{1,0:T(8,128)S(1)}, f32[384,128]{1,0:T(8,128)S(1)}, u32[]{:S(2)}, u32[]{:S(2)}) %collective-permute-start) | collective-permute-done | bytes 196640 | tf_op jit(solution)/shard_map/ppermute | solution.py:280
  19.8 0.0 collective-permute-done.1
  19.8 2.0 %collective-permute-start.2 = (f32[384,128]{1,0:T(8,128)S(1)}, f32[384,128]{1,0:T(8,128)S(1)}, u32[]{:S(2)}, u32[]{:S(2)}) collective-permute-start(f32[384,128]{1,0:T(8,128)S(1)} %add_add_fusion), channel_id=1, source_target_pairs={{0,1},{1,0},{2,3},{3,2},{4,5},{5,4},{6,7},{7,6},{8,9},{9,8},{10,11... | collective-permute-start | bytes 589832 | tf_op jit(solution)/shard_map/ppermute | solution.py:252
  21.8 6.8 %collective-permute-done.5 = f32[512,128]{1,0:T(8,128)S(1)} collective-permute-done((f32[512,128]{1,0:T(8,128)S(1)}, f32[512,128]{1,0:T(8,128)S(1)}, u32[]{:S(2)}, u32[]{:S(2)}) %collective-permute-start.5) | collective-permute-done | bytes 262176 | tf_op jit(solution)/shard_map/ppermute | solution.py:252
  28.7 2.0 %collective-permute-start.9 = (f32[256,128]{1,0:T(8,128)S(1)}, f32[256,128]{1,0:T(8,128)S(1)}, u32[]{:S(2)}, u32[]{:S(2)}) collective-permute-start(f32[256,128]{1,0:T(8,128)S(1)} %get-tuple-element.19), channel_id=1, source_target_pairs={{2,0},{4,2},{6,4},{8,6},{10,8},{12,10},{14,12},{16,14},{18,16},{20... | collective-permute-start | bytes 393224 | tf_op jit(solution)/shard_map/ppermute | solution.py:289
  30.7 0.0 collective-permute-start.8
  30.7 0.1 collective-permute-done.2
  30.8 4.4 %collective-permute-start.7 = (f32[384,128]{1,0:T(8,128)S(1)}, f32[384,128]{1,0:T(8,128)S(1)}, u32[]{:S(2)}, u32[]{:S(2)}) collective-permute-start(f32[384,128]{1,0:T(8,128)S(1)} %add.58.refs_0_), channel_id=1, source_target_pairs={{2,0},{4,2},{6,4},{8,6},{10,8},{12,10},{14,12},{16,14},{18,16},{20... | collective-permute-start | bytes 589832 | tf_op jit(solution)/shard_map/ppermute | solution.py:286
  35.2 0.0 collective-permute-start.6
  35.2 0.1 convert_reduce_fusion
  35.3 0.7 %pad_add_fusion.meta_ref = s32[14]{0:T(128)S(1)} fusion(s32[6]{0:T(128)S(1)} %get-tuple-element.22, s32[6]{0:T(128)S(1)} %convert_reduce_fusion, s32[1]{0:T(128)} %bitcast.2, s32[1]{0:T(128)} %bitcast.1), kind=kLoop, calls=%fused_computation.11 | loop fusion | flops 42 | bytes 112 | tf_op jit(solution)/shard_map/concatenate | solution.py:309
  36.1 0.0 collective-permute-done.10.refs_7_
  36.1 0.0 collective-permute-done.9.refs_5_
  36.1 1.7 %collective-permute-done.8.refs_4_ = f32[256,128]{1,0:T(8,128)S(1)} collective-permute-done((f32[256,128]{1,0:T(8,128)S(1)}, f32[256,128]{1,0:T(8,128)S(1)}, u32[]{:S(2)}, u32[]{:S(2)}) %collective-permute-start.8) | collective-permute-done | bytes 131104 | tf_op jit(solution)/shard_map/ppermute | solution.py:288
  37.8 0.6 %collective-permute-done.7.refs_3_ = f32[384,128]{1,0:T(8,128)S(1)} collective-permute-done((f32[384,128]{1,0:T(8,128)S(1)}, f32[384,128]{1,0:T(8,128)S(1)}, u32[]{:S(2)}, u32[]{:S(2)}) %collective-permute-start.7) | collective-permute-done | bytes 196640 | tf_op jit(solution)/shard_map/ppermute | solution.py:286
  38.4 4.6 %collective-permute-done.6.refs_2_ = f32[384,128]{1,0:T(8,128)S(1)} collective-permute-done((f32[384,128]{1,0:T(8,128)S(1)}, f32[384,128]{1,0:T(8,128)S(1)}, u32[]{:S(2)}, u32[]{:S(2)}) %collective-permute-start.6) | collective-permute-done | bytes 196640 | tf_op jit(solution)/shard_map/ppermute | solution.py:285
  43.0 6.4 %sign.14 = f32[768,128]{1,0:T(8,128)} custom-call(s32[14]{0:T(128)S(1)} %pad_add_fusion.meta_ref, f32[384,128]{1,0:T(8,128)S(1)} %add.58.refs_0_, f32[512,128]{1,0:T(8,128)S(1)} %add.60.refs_1_, f32[384,128]{1,0:T(8,128)S(1)} %collective-permute-done.6.refs_2_, f32[384,128]{1,0:T(8,128)S(1)} %collective-permute-done.7.refs_3_, ...), custom_call_target="tpu_custom_call" | custom-call | flops 3623878656 | bytes 2359296 | tf_op jit(solution)/shard_map/sign/pallas_call | solution.py:220
  (5 shorter events, 0.1 us)
Async XLA Ops:
  0.0 0.7 %copy-start = (f32[1,1,2048]{2,1,0:T(1,128)S(1)}, f32[1,1,2048]{2,1,0:T(1,128)}, u32[]{:S(2)}) copy-start(f32[1,1,2048]{2,1,0:T(1,128)} %potential_ref.1) | copy-start | bytes 24580
  0.7 17.9 %copy-start.1 = (s32[1,1,6]{2,1,0:T(1,128)S(1)}, s32[1,1,6]{2,1,0:T(1,128)}, u32[]{:S(2)}) copy-start(s32[1,1,6]{2,1,0:T(1,128)} %param.5) | copy-start | bytes 76
  6.4 11.9 %collective-permute-start.3 = (f32[256,128]{1,0:T(8,128)S(1)}, f32[256,128]{1,0:T(8,128)S(1)}, u32[]{:S(2)}, u32[]{:S(2)}) collective-permute-start(f32[256,128]{1,0:T(8,128)S(1)} %get-tuple-element.16), channel_id=1, source_target_pairs={{0,2},{2,4},{4,6},{6,8},{8,10},{10,12},{12,14},{14,16},{16,18},{18... | collective-permute-start | bytes 393224 | tf_op jit(solution)/shard_map/ppermute | solution.py:281
  7.0 11.4 %collective-permute-start.4 = (f32[256,128]{1,0:T(8,128)S(1)}, f32[256,128]{1,0:T(8,128)S(1)}, u32[]{:S(2)}, u32[]{:S(2)}) collective-permute-start(f32[256,128]{1,0:T(8,128)S(1)} %get-tuple-element.17), channel_id=1, source_target_pairs={{2,0},{4,2},{6,4},{8,6},{10,8},{12,10},{14,12},{16,14},{18,16},{20... | collective-permute-start | bytes 393224 | tf_op jit(solution)/shard_map/ppermute | solution.py:281
  12.0 7.8 %collective-permute-start = (f32[384,128]{1,0:T(8,128)S(1)}, f32[384,128]{1,0:T(8,128)S(1)}, u32[]{:S(2)}, u32[]{:S(2)}) collective-permute-start(f32[384,128]{1,0:T(8,128)S(1)} %get-tuple-element.13), channel_id=1, source_target_pairs={{0,2},{2,4},{4,6},{6,8},{8,10},{10,12},{12,14},{14,16},{16,18},{18... | collective-permute-start | bytes 589832 | tf_op jit(solution)/shard_map/ppermute | solution.py:280
  12.0 7.8 %collective-permute-start.1 = (f32[384,128]{1,0:T(8,128)S(1)}, f32[384,128]{1,0:T(8,128)S(1)}, u32[]{:S(2)}, u32[]{:S(2)}) collective-permute-start(f32[384,128]{1,0:T(8,128)S(1)} %get-tuple-element.14), channel_id=1, source_target_pairs={{2,0},{4,2},{6,4},{8,6},{10,8},{12,10},{14,12},{16,14},{18,16},{20... | collective-permute-start | bytes 589832 | tf_op jit(solution)/shard_map/ppermute | solution.py:280
  16.5 19.6 %collective-permute-start.10 = (f32[512,128]{1,0:T(8,128)S(1)}, f32[512,128]{1,0:T(8,128)S(1)}, u32[]{:S(2)}, u32[]{:S(2)}) collective-permute-start(f32[512,128]{1,0:T(8,128)S(1)} %get-tuple-element.18.refs_6_), channel_id=1, source_target_pairs={{0,1},{1,0},{2,3},{3,2},{4,5},{5,4},{6,7},{7,6},{8,9},{9,8},{10,11... | collective-permute-start | bytes 786440 | tf_op jit(solution)/shard_map/ppermute | solution.py:252
  18.4 10.2 %collective-permute-start.5 = (f32[512,128]{1,0:T(8,128)S(1)}, f32[512,128]{1,0:T(8,128)S(1)}, u32[]{:S(2)}, u32[]{:S(2)}) collective-permute-start(f32[512,128]{1,0:T(8,128)S(1)} %maximum_add_fusion), channel_id=1, source_target_pairs={{0,1},{1,0},{2,3},{3,2},{4,5},{5,4},{6,7},{7,6},{8,9},{9,8},{10,11... | collective-permute-start | bytes 786440 | tf_op jit(solution)/shard_map/ppermute | solution.py:252
  19.8 10.9 %collective-permute-start.2 = (f32[384,128]{1,0:T(8,128)S(1)}, f32[384,128]{1,0:T(8,128)S(1)}, u32[]{:S(2)}, u32[]{:S(2)}) collective-permute-start(f32[384,128]{1,0:T(8,128)S(1)} %add_add_fusion), channel_id=1, source_target_pairs={{0,1},{1,0},{2,3},{3,2},{4,5},{5,4},{6,7},{7,6},{8,9},{9,8},{10,11... | collective-permute-start | bytes 589832 | tf_op jit(solution)/shard_map/ppermute | solution.py:252
  28.7 7.4 %collective-permute-start.9 = (f32[256,128]{1,0:T(8,128)S(1)}, f32[256,128]{1,0:T(8,128)S(1)}, u32[]{:S(2)}, u32[]{:S(2)}) collective-permute-start(f32[256,128]{1,0:T(8,128)S(1)} %get-tuple-element.19), channel_id=1, source_target_pairs={{2,0},{4,2},{6,4},{8,6},{10,8},{12,10},{14,12},{16,14},{18,16},{20... | collective-permute-start | bytes 393224 | tf_op jit(solution)/shard_map/ppermute | solution.py:289
  30.7 7.1 %collective-permute-start.8 = (f32[256,128]{1,0:T(8,128)S(1)}, f32[256,128]{1,0:T(8,128)S(1)}, u32[]{:S(2)}, u32[]{:S(2)}) collective-permute-start(f32[256,128]{1,0:T(8,128)S(1)} %get-tuple-element.20), channel_id=1, source_target_pairs={{0,2},{2,4},{4,6},{6,8},{8,10},{10,12},{12,14},{14,16},{16,18},{18... | collective-permute-start | bytes 393224 | tf_op jit(solution)/shard_map/ppermute | solution.py:288
  30.8 7.6 %collective-permute-start.7 = (f32[384,128]{1,0:T(8,128)S(1)}, f32[384,128]{1,0:T(8,128)S(1)}, u32[]{:S(2)}, u32[]{:S(2)}) collective-permute-start(f32[384,128]{1,0:T(8,128)S(1)} %add.58.refs_0_), channel_id=1, source_target_pairs={{2,0},{4,2},{6,4},{8,6},{10,8},{12,10},{14,12},{16,14},{18,16},{20... | collective-permute-start | bytes 589832 | tf_op jit(solution)/shard_map/ppermute | solution.py:286
  35.2 7.8 %collective-permute-start.6 = (f32[384,128]{1,0:T(8,128)S(1)}, f32[384,128]{1,0:T(8,128)S(1)}, u32[]{:S(2)}, u32[]{:S(2)}) collective-permute-start(f32[384,128]{1,0:T(8,128)S(1)} %add.58.refs_0_), channel_id=1, source_target_pairs={{0,2},{2,4},{4,6},{6,8},{8,10},{10,12},{12,14},{14,16},{16,18},{18... | collective-permute-start | bytes 589832 | tf_op jit(solution)/shard_map/ppermute | solution.py:285

commit v2 on v1

--- a/solution.py
+++ b/solution.py
@@ -41,12 +41,14 @@
     return place(below_part, 0) + place(centre_part, 1) + place(above_part, 2)
 
 
-def product_kernel(outputs, lines, chunks, start_ref, values_ref, potential_ref, *refs):
-    outs, (held, turned, total, sems) = refs[:-4], refs[-4:]
+def product_kernel(both_pairs, lines, chunks, start_ref, values_ref, potential_ref, *refs):
+    outs, (held, turned, total, means, levels, sems, level_sem) = refs[:-7], refs[-7:]
     depth, size = held.shape[1:]
     wide = size // REACH
     block = wide // lines
     start = start_ref[0]
+    level_copy = pltpu.make_async_copy(potential_ref.at[0], levels, level_sem)
+    level_copy.start()
     copies = []
     for c in range(chunks):
         for a in range(REACH):
@@ -63,47 +65,59 @@
     def prepare(c):
         for a in range(REACH):
             copies[c * REACH + a].wait()
-        level = potential_ref[0, :, c * depth : (c + 1) * depth]
+        level = levels[:, c * depth : (c + 1) * depth]
         turned[c % 2] = (held[c].T.astype(F32) * level).astype(BF16)
 
+    level_copy.wait()
     prepare(0)
     for c in range(chunks):
         if c + 1 < chunks:
             prepare(c + 1)
-        for a in range(REACH):
-            columns = pl.ds(a * wide, wide)
-            part = jnp.dot(turned[c % 2], held[c, :, columns], preferred_element_type=F32)
-            total[:, columns] = part if c == 0 else total[:, columns] + part
-
-    def mean(i, j):
+        for n in range(0, size, 256):
+            for m in range(0, size, 768):
+                here = pl.ds(m, 768), pl.ds(n, 256)
+                part = jnp.dot(
+                    turned[c % 2, here[0], :], held[c, :, here[1]], preferred_element_type=F32
+                )
+                total[here] = part if c == 0 else total[here] + part
+
+    wanted = sorted({pair for lists in both_pairs for pairs in lists for pair in pairs})
+    for n, (i, j) in enumerate(wanted):
         rows, columns = pl.ds(i * block, block), pl.ds(j * block, block)
-        return 0.5 * (total[rows, columns] + total[columns, rows].T)
-
-    for out, pairs in zip(outs, outputs):
-        for n, (i, j) in enumerate(pairs):
-            out[n * block : (n + 1) * block, :] = mean(i, j)
-
-
-def local_products(values, potential, start, outputs, lines):
+        means[n] = 0.5 * (total[rows, columns] + total[columns, rows].T)
+    odd = start_ref[1] == 1
+    for out, evens, odds in zip(outs, *both_pairs):
+        for n, (even_pair, odd_pair) in enumerate(zip(evens, odds)):
+            index = wanted.index(even_pair)
+            if even_pair != odd_pair:
+                index = jnp.where(odd, wanted.index(odd_pair), index)
+            out[n * block : (n + 1) * block, :] = means[index]
+
+
+def local_products(values, potential, start, both_pairs, lines):
     points, width = values.shape[2:]
     block = width // (REACH * REACH)
     size = block * lines * REACH
-    chunks = 4
+    chunks = 1
     vmem = pl.BlockSpec(memory_space=pltpu.VMEM)
+    counts = [len(pairs) for pairs in both_pairs[0]]
     return pl.pallas_call(
-        functools.partial(product_kernel, outputs, lines, chunks),
-        out_shape=[jax.ShapeDtypeStruct((len(pairs) * block, block), F32) for pairs in outputs],
+        functools.partial(product_kernel, both_pairs, lines, chunks),
+        out_shape=[jax.ShapeDtypeStruct((n * block, block), F32) for n in counts],
         in_specs=[
             pl.BlockSpec(memory_space=pltpu.SMEM),
             pl.BlockSpec(memory_space=pltpu.HBM),
-            vmem,
+            pl.BlockSpec(memory_space=pltpu.HBM),
         ],
-        out_specs=[vmem] * len(outputs),
+        out_specs=[vmem] * len(counts),
         scratch_shapes=[
             pltpu.VMEM((chunks, points // chunks, size), BF16),
             pltpu.VMEM((2, size, points // chunks), BF16),
             pltpu.VMEM((size, size), F32),
+            pltpu.VMEM((REACH * REACH * lines * lines, block, block), F32),
+            pltpu.VMEM((1, points), F32),
             pltpu.SemaphoreType.DMA((chunks, REACH)),
+            pltpu.SemaphoreType.DMA,
         ],
         compiler_params=pltpu.CompilerParams(vmem_limit_bytes=LOADING_BYTES),
         cost_estimate=pl.CostEstimate(
@@ -124,14 +138,16 @@
         == lax.broadcasted_iota(jnp.int32, (block, block), 1)
     ).astype(F32)
     dot = functools.partial(jnp.dot, preferred_element_type=F32)
+    odd = meta_ref[2 + 2 * slots] == 1
 
     def at(i, width=tile):
         return pl.ds(i * width, width)
 
     def read(k, l):
         total = None
-        for piece, n in place(k, l):
-            part = pieces[piece][n * block : (n + 1) * block, :]
+        for choices in place(k, l):
+            parts = [pieces[piece][n * block : (n + 1) * block, :] for piece, n in choices]
+            part = parts[0] if len(parts) == 1 else jnp.where(odd, parts[1], parts[0])
             total = part if total is None else total + part
         return total
 
@@ -148,22 +164,24 @@
         for i in range(j):
             to[at(j), at(i)] = upper[i * tile : (i + 1) * tile].T
 
-    trace = sum(jnp.sum(read(k, k) * eye) * used[k] for k in range(slots))
+    trace = jnp.sum(sum(fold(read(k, k) * eye) * used[k] for k in range(slots)))
     mean_level = trace / live_count
     square_sum = jnp.zeros((8, block), F32)
     for k in range(slots):
         for l in range(k, slots):
             part = read(k, l)
-            part = (mean_level * eye - part if k == l else -part) * (used[k] * used[l])
+            if k == l:
+                part = part - mean_level * eye
+            part = part * -(used[k] * used[l])
             square_sum = square_sum + fold(part * part) * (1.0 if k == l else 2.0)
             rows, columns = at(k, block), at(l, block)
             xf[rows, columns] = part
-            xb[rows, columns] = part.astype(BF16)
+            short = part.astype(BF16)
+            xb[rows, columns] = short
             if k < l:
-                mirror = part.T
-                xb[columns, rows] = mirror.astype(BF16)
+                xb[columns, rows] = short.T
                 if k // per_tile == l // per_tile:
-                    xf[columns, rows] = mirror
+                    xf[columns, rows] = part.T
     norm = lax.rsqrt(jnp.full((1, 1), jnp.sum(square_sum) + 1e-06, F32)) * jnp.sqrt(
         jnp.full((1, 1), live_count, F32)
     )
@@ -202,8 +220,12 @@
     def thin(v):
         high = v.astype(BF16)
         low = (v - high.astype(F32)).astype(BF16)
-        both = dot(yb[...], jnp.concatenate([high, low], axis=1))
-        return both[:, :block] + both[:, block:]
+        halves = []
+        for n, pair in enumerate(((high, low), (low, high))):
+            rows = pl.ds(n * size // 2, size // 2)
+            both = dot(yb[rows, :], jnp.concatenate(pair, axis=1))
+            halves.append(both[:, :block] + both[:, block:])
+        return jnp.concatenate(halves, axis=0)
 
     xf[:, :block] = 1.5 * columns - 0.5 * thin(thin(columns))
     for s in range(slots):
@@ -241,72 +263,78 @@
 def shards_dense_line(basis_values, potential, block_lists):
     codes = block_lists[0, 0]
     lines = lax.axis_size("grid")
-    position = lax.axis_index("grid")
+    position = lax.axis_index("grid").astype(jnp.int32)
+    parity = (lax.axis_index("atoms") % 2).astype(jnp.int32)
     block = basis_values.shape[3] // (REACH * REACH)
     slots = REACH * lines
-    up, down = ring(lax.axis_size("atoms"), True)
+    regions = lax.axis_size("atoms")
+    far = [(i, (i + 1 if i % 2 else i - 1) % regions) for i in range(regions)]
+    near = [(i, i - 1 if i % 2 else i + 1) for i in range(regions)]
     line_shifts = [[(i, (i + s) % lines) for i in range(lines)] for s in range(1, lines)]
-    start = (1 - position).astype(jnp.int32)[None]
+    start = jnp.stack([1 - position, parity])
+
+    def sent(part, axis, pairs):
+        return lax.ppermute(part, axis, pairs)
 
     def line_parts(part):
-        return [lax.ppermute(part, "grid", shift) for shift in line_shifts]
+        return [sent(part, "grid", shift) for shift in line_shifts]
 
     half = lines // 2
     triangle = [(r, q) for r in range(lines) for q in range(r, lines)]
+    strip = [(r, q) for r in range(half) for q in range(lines)]
 
     def within(a):
         return [(a * lines + r, a * lines + q) for r, q in triangle]
 
-    def across(a, b, rows):
-        return [(a * lines + r, b * lines + q) for r in rows for q in range(lines)]
-
-    early, late = range(half), range(half, lines)
-    up_own, up_side, down_own, down_side, outer, own, side = local_products(
-        basis_values,
-        potential,
-        start,
-        (
-            within(2),
-            across(1, 2, early),
-            within(0),
-            across(0, 1, late),
-            across(0, 2, range(lines)),
+    def across(a, late):
+        first = half if late else 0
+        return [(a * lines + first + r, (a + 1) * lines + q) for r, q in strip]
+
+    def pairs_of(odd):
+        return (
+            within(2 * odd),
+            within(2 - 2 * odd),
+            across(odd, not odd),
+            across(1 - odd, odd),
             within(1),
-            across(0, 1, early) + across(1, 2, late),
-        ),
-        lines,
+            across(odd, odd) + across(1 - odd, not odd),
+            [(r, 2 * lines + q) for r in range(lines) for q in range(lines)],
+        )
+
+    own_to_far, own_to_near, side_to_far, side_to_near, own, side, outer = local_products(
+        basis_values, potential, start, (pairs_of(0), pairs_of(1)), lines
     )
     outer_parts = [outer] + line_parts(outer)
-    own = own + lax.ppermute(up_own, "atoms", up) + lax.ppermute(down_own, "atoms", down)
-    up_side, down_side = lax.ppermute(up_side, "atoms", up), lax.ppermute(down_side, "atoms", down)
-    side = side + jnp.concatenate([up_side, down_side])
+    own = own + sent(own_to_far, "atoms", far) + sent(own_to_near, "atoms", near)
+    side_far, side_near = sent(side_to_far, "atoms", far), sent(side_to_near, "atoms", near)
+    side = side + jnp.concatenate([side_far, side_near])
     own = sum(line_parts(own), own)
     side = sum(line_parts(side), side)
-    below_own = lax.ppermute(own, "atoms", up)
-    above_own = lax.ppermute(own, "atoms", down)
-    cut = half * lines * block
-    below_side = lax.ppermute(side[cut:], "atoms", up)
-    above_side = lax.ppermute(side[:cut], "atoms", down)
-    pieces = [own, side, below_own, above_own, below_side, above_side] + outer_parts
+    own_far = sent(own, "atoms", far)
+    own_near = sent(own, "atoms", near)
+    cut = len(strip) * block
+    side_far = sent(side[:cut], "atoms", far)
+    side_near = sent(side[cut:], "atoms", near)
+    pieces = [own, own_far, own_near, side, side_far, side_near] + outer_parts
 
     def place(k, l):
         (a, r), (b, q) = divmod(k, lines), divmod(l, lines)
         if a == b:
-            return [((2, 0, 3)[a], triangle.index((r, q)))]
+            n = triangle.index((r, q))
+            return [(((1, n), (2, n)), ((0, n),), ((2, n), (1, n)))[a]]
         if b - a == 2:
-            return [(n, r * lines + q) for n in range(6, len(pieces))]
-        if r < half:
-            return [((1, 5)[a], r * lines + q)]
-        if a == 0:
-            return [(4, (r - half) * lines + q)]
-        return [(1, r * lines + q)]
+            return [((piece, r * lines + q),) for piece in range(6, len(pieces))]
+        n = strip.index((r % half, q))
+        kept, given = ((3, n), (3, len(strip) + n)), ((4, n), (5, n))
+        choices = kept if (r < half) == (a == 0) else given
+        return [choices if a == 0 else choices[::-1]]
 
     live = jnp.sum((codes >= 0).astype(jnp.int32))
     source = (codes // REACH) * lines + codes % REACH - 1 + position
     source = jnp.where(codes >= 0, source, -1).astype(jnp.int32)
     blocks = jnp.arange(slots, dtype=jnp.int32)
     used = jnp.sum((source[None, :] == blocks[:, None]).astype(jnp.int32), axis=1)
-    meta = jnp.concatenate([live[None], position[None].astype(jnp.int32), used, source])
+    meta = jnp.concatenate([live[None], position[None], used, source, parity[None]])
     return sign_columns(meta, pieces, place, slots, block, 1)[None, None]
 
 
@@ -339,13 +367,14 @@
     pieces = [submatrix[k, :, k:].transpose(1, 0, 2).reshape(-1, block_size) for k in range(slots)]
     used = (slot_codes >= 0).astype(jnp.int32)
     source = jnp.where(slot_codes >= 0, jnp.arange(slots, dtype=jnp.int32), -1)
-    meta = jnp.concatenate([jnp.sum(used)[None], jnp.zeros((1,), jnp.int32), used, source])
-    return sign_columns(meta, pieces, lambda k, l: [(k, l - k)], slots, block_size, 0)[None, None]
+    none = jnp.zeros((1,), jnp.int32)
+    meta = jnp.concatenate([jnp.sum(used)[None], none, used, source, none])
+    return sign_columns(meta, pieces, lambda k, l: [((k, l - k),)], slots, block_size, 0)[None, None]
 
 
 def solution(mesh):
     placed = (P("atoms", "grid", None, None), P("atoms", "grid", None), P("atoms", "grid", None))
-    dense = mesh.shape["grid"] == 2 and mesh.shape["atoms"] >= 5
+    dense = mesh.shape["grid"] == 2 and mesh.shape["atoms"] % 2 == 0 and mesh.shape["atoms"] > 4
 
     def body(basis_values, potential, block_lists):
         if dense and block_lists.shape[2] == REACH * mesh.shape["grid"]:

time: 49.6 us -> 47.6 us (0.960)
  waiting for transfers between devices: 14.4 us -> 12.8 us
  local copies, waits for them, and re-layouts: 0.72 us -> 1.42 us
  other arithmetic: 1.61 us -> 1 us
    ppermute x11, waiting for transfers between devices: 14.4 us -> 12.8 us  [sent(): return lax.ppermute(part, axis, pairs)]
    concatenate x1 -> x0, other arithmetic: 0.71 us -> none  [shards_dense_line(): jnp.concatenate([live[None], position[None].astype(jnp.int32), used, sour...]
    concatenate x0 -> x1, local copies, waits for them, and re-layouts: none -> 0.7 us  [shards_dense_line(): jnp.concatenate([live[None], position[None], used, source, parity[None]])]
    select_n x0 -> x1, other arithmetic: none -> 0.69 us  [shards_dense_line(): source = jnp.where(codes >= 0, source, -1).astype(jnp.int32)]
    reduce_sum x1 -> x0, other arithmetic: 0.66 us -> none  [shards_dense_line(): live = jnp.sum((codes >= 0).astype(jnp.int32))]
  transfers between devices with their start and end apart: 11 -> 11, of which waited for: 6 -> 5; matrix products, arithmetic and copies ran while one was open for 3% -> 3% of each run, Pallas kernels for 0% -> 0%
where the time goes in v2:
time: 47.6 us; the launch traced here: 47.4 us
  starting transfers between devices  20.3 us (43%)
  waiting for transfers between devices  12.8 us (27%)
  Pallas kernels  11.8 us (25%)
  local copies, waits for them, and re-layouts  1.42 us (3%)
  other arithmetic  1 us (2%)
    ppermute x11, starting transfers between devices, sent(): return lax.ppermute(part, axis, pairs)  20.3 us
    ppermute x11, waiting for transfers between devices, sent(): return lax.ppermute(part, axis, pairs)  12.8 us
    pallas_call x1, Pallas kernels, sign_columns(): pl.pallas_call(functools.partial(sign_kernel, slots, block, own_tile, pla...  6.43 us
    pallas_call x1, Pallas kernels, local_products(): pl.pallas_call(functools.partial(product_kernel, both_pairs, lines, chunk...  5.39 us
  transfers between devices with their start and end apart: 11, of which 5 were waited for; matrix products, arithmetic and copies ran while one was open for 3% of the time, Pallas kernels for 0%

profile of v2, /device:TPU:0, one launch (start us, length us, event | category | flops | bytes accessed | tf_op | source)
XLA Modules:
  0.0 47.4 jit_solution(4942882361401627798)
XLA Ops:
  0.0 0.1 pad_add_fusion.start_ref
  0.1 0.0 copy-start
  0.1 0.7 %copy-done = f32[1,1,2048]{2,1,0:T(1,128)S(1)} copy-done((f32[1,1,2048]{2,1,0:T(1,128)S(1)}, f32[1,1,2048]{2,1,0:T(1,128)}, u32[]{:S(2)}) %copy-start) | copy-done | bytes 8216
  0.8 0.0 copy-start.1
  0.8 5.4 %products.1 = (f32[384,128]{1,0:T(8,128)S(1)}, f32[384,128]{1,0:T(8,128)S(1)}, f32[256,128]{1,0:T(8,128)S(1)}, f32[256,128]{1,0:T(8,128)S(1)}, f32[384,128]{1,0:...) custom-call(s32[2]{0:T(128)S(1)} %pad_add_fusion.start_ref, bf16[1,1,2048,1152]{3,2,1,0:T(8,128)(2,1)} %values_ref.1, ...), custom_call_target="tpu_custom_call" | custom-call | flops 2415919104 | bytes 3145728 | tf_op jit(solution)/shard_map/products/pallas_call | solution.py:104
  6.2 5.5 %collective-permute-start.5 = (f32[256,128]{1,0:T(8,128)S(1)}, f32[256,128]{1,0:T(8,128)S(1)}, u32[]{:S(2)}, u32[]{:S(2)}) collective-permute-start(f32[256,128]{1,0:T(8,128)S(1)} %get-tuple-element.16), channel_id=1, source_target_pairs={{0,30},{2,4},{4,2},{6,8},{8,6},{10,12},{12,10},{14,16},{16,14},{18... | collective-permute-start | bytes 393224 | tf_op jit(solution)/shard_map/ppermute | solution.py:277
  11.7 0.0 collective-permute-start.6
  11.7 0.7 %collective-permute-start = (f32[384,128]{1,0:T(8,128)S(1)}, f32[384,128]{1,0:T(8,128)S(1)}, u32[]{:S(2)}, u32[]{:S(2)}) collective-permute-start(f32[384,128]{1,0:T(8,128)S(1)} %get-tuple-element.13), channel_id=1, source_target_pairs={{0,30},{2,4},{4,2},{6,8},{8,6},{10,12},{12,10},{14,16},{16,14},{18... | collective-permute-start | bytes 589832 | tf_op jit(solution)/shard_map/ppermute | solution.py:277
  12.4 0.0 collective-permute-start.1
  12.4 1.9 %collective-permute-done.5 = f32[256,128]{1,0:T(8,128)S(1)} collective-permute-done((f32[256,128]{1,0:T(8,128)S(1)}, f32[256,128]{1,0:T(8,128)S(1)}, u32[]{:S(2)}, u32[]{:S(2)}) %collective-permute-start.5) | collective-permute-done | bytes 131104 | tf_op jit(solution)/shard_map/ppermute | solution.py:277
  14.3 0.0 collective-permute-done.6
  14.4 2.1 %collective-permute-start.7 = (f32[512,128]{1,0:T(8,128)S(1)}, f32[512,128]{1,0:T(8,128)S(1)}, u32[]{:S(2)}, u32[]{:S(2)}) collective-permute-start(f32[512,128]{1,0:T(8,128)S(1)} %maximum_add_fusion), channel_id=1, source_target_pairs={{0,1},{1,0},{2,3},{3,2},{4,5},{5,4},{6,7},{7,6},{8,9},{9,8},{10,11... | collective-permute-start | bytes 786440 | tf_op jit(solution)/shard_map/ppermute | solution.py:277
  16.4 0.1 collective-permute-start.10
  16.5 3.1 %collective-permute-done = f32[384,128]{1,0:T(8,128)S(1)} collective-permute-done((f32[384,128]{1,0:T(8,128)S(1)}, f32[384,128]{1,0:T(8,128)S(1)}, u32[]{:S(2)}, u32[]{:S(2)}) %collective-permute-start) | collective-permute-done | bytes 196640 | tf_op jit(solution)/shard_map/ppermute | solution.py:277
  19.6 0.0 collective-permute-done.1
  19.6 1.6 %collective-permute-start.2 = (f32[384,128]{1,0:T(8,128)S(1)}, f32[384,128]{1,0:T(8,128)S(1)}, u32[]{:S(2)}, u32[]{:S(2)}) collective-permute-start(f32[384,128]{1,0:T(8,128)S(1)} %add_add_fusion), channel_id=1, source_target_pairs={{0,1},{1,0},{2,3},{3,2},{4,5},{5,4},{6,7},{7,6},{8,9},{9,8},{10,11... | collective-permute-start | bytes 589832 | tf_op jit(solution)/shard_map/ppermute | solution.py:277
  21.2 2.4 %collective-permute-done.7 = f32[512,128]{1,0:T(8,128)S(1)} collective-permute-done((f32[512,128]{1,0:T(8,128)S(1)}, f32[512,128]{1,0:T(8,128)S(1)}, u32[]{:S(2)}, u32[]{:S(2)}) %collective-permute-start.7) | collective-permute-done | bytes 262176 | tf_op jit(solution)/shard_map/ppermute | solution.py:277
  23.7 0.1 collective-permute-start.9
  23.8 4.0 %collective-permute-start.8 = (f32[256,128]{1,0:T(8,128)S(1)}, f32[256,128]{1,0:T(8,128)S(1)}, u32[]{:S(2)}, u32[]{:S(2)}) collective-permute-start(f32[256,128]{1,0:T(8,128)S(1)} %get-tuple-element.20), channel_id=1, source_target_pairs={{0,30},{2,4},{4,2},{6,8},{8,6},{10,12},{12,10},{14,16},{16,14},{18... | collective-permute-start | bytes 393224 | tf_op jit(solution)/shard_map/ppermute | solution.py:277
  27.8 3.5 %collective-permute-done.2 = f32[384,128]{1,0:T(8,128)S(1)} collective-permute-done((f32[384,128]{1,0:T(8,128)S(1)}, f32[384,128]{1,0:T(8,128)S(1)}, u32[]{:S(2)}, u32[]{:S(2)}) %collective-permute-start.2) | collective-permute-done | bytes 196640 | tf_op jit(solution)/shard_map/ppermute | solution.py:277
  31.4 0.1 collective-permute-start.4
  31.4 6.1 %collective-permute-start.3 = (f32[384,128]{1,0:T(8,128)S(1)}, f32[384,128]{1,0:T(8,128)S(1)}, u32[]{:S(2)}, u32[]{:S(2)}) collective-permute-start(f32[384,128]{1,0:T(8,128)S(1)} %add.63.refs_0_), channel_id=1, source_target_pairs={{0,30},{2,4},{4,2},{6,8},{8,6},{10,12},{12,10},{14,16},{16,14},{18... | collective-permute-start | bytes 589832 | tf_op jit(solution)/shard_map/ppermute | solution.py:277
  37.6 0.0 copy-done.1
  37.6 0.7 %bitcast_select_fusion = (s32[6]{0:T(128)S(1)}, s32[]{:T(128)}) fusion(s32[1,1,6]{2,1,0:T(1,128)S(1)} %copy-done.1, s32[]{:T(128)} %axis_index.22), kind=kLoop, calls=%fused_computation.6 | loop fusion | flops 119 | bytes 56 | tf_op jit(solution)/shard_map/jit(_where)/select_n | solution.py:334
  38.3 0.1 convert_reduce_fusion
  38.4 0.7 %concatenate.6.meta_ref = s32[15]{0:T(128)S(1)} concatenate(s32[1]{0:T(128)} %bitcast.1, s32[1]{0:T(128)} %bitcast.2, s32[6]{0:T(128)S(1)} %convert_reduce_fusion, s32[6]{0:T(128)S(1)} %get-tuple-element.21, s32[1]{0:T(128)} %bitcast.6), dimensions={0} | concatenate | bytes 120 | tf_op jit(solution)/shard_map/concatenate | solution.py:337
  39.1 0.0 collective-permute-done.10.refs_7_
  39.1 0.0 collective-permute-done.9.refs_5_
  39.1 0.0 collective-permute-done.8.refs_4_
  39.1 0.0 collective-permute-done.4.refs_2_
  39.1 1.8 %collective-permute-done.3.refs_1_ = f32[384,128]{1,0:T(8,128)S(1)} collective-permute-done((f32[384,128]{1,0:T(8,128)S(1)}, f32[384,128]{1,0:T(8,128)S(1)}, u32[]{:S(2)}, u32[]{:S(2)}) %collective-permute-start.3) | collective-permute-done | bytes 196640 | tf_op jit(solution)/shard_map/ppermute | solution.py:277
  40.9 6.4 %sign.14 = f32[768,128]{1,0:T(8,128)} custom-call(s32[15]{0:T(128)S(1)} %concatenate.6.meta_ref, f32[384,128]{1,0:T(8,128)S(1)} %add.63.refs_0_, f32[384,128]{1,0:T(8,128)S(1)} %collective-permute-done.3.refs_1_, f32[384,128]{1,0:T(8,128)S(1)} %collective-permute-done.4.refs_2_, f32[512,128]{1,0:T(8,128)S(1)} %add.65.refs_3_, ...), custom_call_target="tpu_custom_call" | custom-call | flops 3623878656 | bytes 2359296 | tf_op jit(solution)/shard_map/sign/pallas_call | solution.py:242
  (5 shorter events, 0.1 us)
Async XLA Ops:
  0.1 0.7 %copy-start = (f32[1,1,2048]{2,1,0:T(1,128)S(1)}, f32[1,1,2048]{2,1,0:T(1,128)}, u32[]{:S(2)}) copy-start(f32[1,1,2048]{2,1,0:T(1,128)} %potential_ref.1) | copy-start | bytes 24580
  0.8 36.8 %copy-start.1 = (s32[1,1,6]{2,1,0:T(1,128)S(1)}, s32[1,1,6]{2,1,0:T(1,128)}, u32[]{:S(2)}) copy-start(s32[1,1,6]{2,1,0:T(1,128)} %param.5) | copy-start | bytes 76
  6.2 8.2 %collective-permute-start.5 = (f32[256,128]{1,0:T(8,128)S(1)}, f32[256,128]{1,0:T(8,128)S(1)}, u32[]{:S(2)}, u32[]{:S(2)}) collective-permute-start(f32[256,128]{1,0:T(8,128)S(1)} %get-tuple-element.16), channel_id=1, source_target_pairs={{0,30},{2,4},{4,2},{6,8},{8,6},{10,12},{12,10},{14,16},{16,14},{18... | collective-permute-start | bytes 393224 | tf_op jit(solution)/shard_map/ppermute | solution.py:277
  11.7 2.7 %collective-permute-start.6 = (f32[256,128]{1,0:T(8,128)S(1)}, f32[256,128]{1,0:T(8,128)S(1)}, u32[]{:S(2)}, u32[]{:S(2)}) collective-permute-start(f32[256,128]{1,0:T(8,128)S(1)} %get-tuple-element.17), channel_id=1, source_target_pairs={{0,2},{2,0},{4,6},{6,4},{8,10},{10,8},{12,14},{14,12},{16,18},{18,... | collective-permute-start | bytes 393224 | tf_op jit(solution)/shard_map/ppermute | solution.py:277
  11.7 7.9 %collective-permute-start = (f32[384,128]{1,0:T(8,128)S(1)}, f32[384,128]{1,0:T(8,128)S(1)}, u32[]{:S(2)}, u32[]{:S(2)}) collective-permute-start(f32[384,128]{1,0:T(8,128)S(1)} %get-tuple-element.13), channel_id=1, source_target_pairs={{0,30},{2,4},{4,2},{6,8},{8,6},{10,12},{12,10},{14,16},{16,14},{18... | collective-permute-start | bytes 589832 | tf_op jit(solution)/shard_map/ppermute | solution.py:277
  12.4 7.1 %collective-permute-start.1 = (f32[384,128]{1,0:T(8,128)S(1)}, f32[384,128]{1,0:T(8,128)S(1)}, u32[]{:S(2)}, u32[]{:S(2)}) collective-permute-start(f32[384,128]{1,0:T(8,128)S(1)} %get-tuple-element.14), channel_id=1, source_target_pairs={{0,2},{2,0},{4,6},{6,4},{8,10},{10,8},{12,14},{14,12},{16,18},{18,... | collective-permute-start | bytes 589832 | tf_op jit(solution)/shard_map/ppermute | solution.py:277
  14.4 9.2 %collective-permute-start.7 = (f32[512,128]{1,0:T(8,128)S(1)}, f32[512,128]{1,0:T(8,128)S(1)}, u32[]{:S(2)}, u32[]{:S(2)}) collective-permute-start(f32[512,128]{1,0:T(8,128)S(1)} %maximum_add_fusion), channel_id=1, source_target_pairs={{0,1},{1,0},{2,3},{3,2},{4,5},{5,4},{6,7},{7,6},{8,9},{9,8},{10,11... | collective-permute-start | bytes 786440 | tf_op jit(solution)/shard_map/ppermute | solution.py:277
  16.4 22.7 %collective-permute-start.10 = (f32[512,128]{1,0:T(8,128)S(1)}, f32[512,128]{1,0:T(8,128)S(1)}, u32[]{:S(2)}, u32[]{:S(2)}) collective-permute-start(f32[512,128]{1,0:T(8,128)S(1)} %get-tuple-element.18.refs_6_), channel_id=1, source_target_pairs={{0,1},{1,0},{2,3},{3,2},{4,5},{5,4},{6,7},{7,6},{8,9},{9,8},{10,11... | collective-permute-start | bytes 786440 | tf_op jit(solution)/shard_map/ppermute | solution.py:277
  19.6 11.7 %collective-permute-start.2 = (f32[384,128]{1,0:T(8,128)S(1)}, f32[384,128]{1,0:T(8,128)S(1)}, u32[]{:S(2)}, u32[]{:S(2)}) collective-permute-start(f32[384,128]{1,0:T(8,128)S(1)} %add_add_fusion), channel_id=1, source_target_pairs={{0,1},{1,0},{2,3},{3,2},{4,5},{5,4},{6,7},{7,6},{8,9},{9,8},{10,11... | collective-permute-start | bytes 589832 | tf_op jit(solution)/shard_map/ppermute | solution.py:277
  23.7 15.4 %collective-permute-start.9 = (f32[256,128]{1,0:T(8,128)S(1)}, f32[256,128]{1,0:T(8,128)S(1)}, u32[]{:S(2)}, u32[]{:S(2)}) collective-permute-start(f32[256,128]{1,0:T(8,128)S(1)} %get-tuple-element.19), channel_id=1, source_target_pairs={{0,2},{2,0},{4,6},{6,4},{8,10},{10,8},{12,14},{14,12},{16,18},{18,... | collective-permute-start | bytes 393224 | tf_op jit(solution)/shard_map/ppermute | solution.py:277
  23.8 15.3 %collective-permute-start.8 = (f32[256,128]{1,0:T(8,128)S(1)}, f32[256,128]{1,0:T(8,128)S(1)}, u32[]{:S(2)}, u32[]{:S(2)}) collective-permute-start(f32[256,128]{1,0:T(8,128)S(1)} %get-tuple-element.20), channel_id=1, source_target_pairs={{0,30},{2,4},{4,2},{6,8},{8,6},{10,12},{12,10},{14,16},{16,14},{18... | collective-permute-start | bytes 393224 | tf_op jit(solution)/shard_map/ppermute | solution.py:277
  31.4 7.8 %collective-permute-start.4 = (f32[384,128]{1,0:T(8,128)S(1)}, f32[384,128]{1,0:T(8,128)S(1)}, u32[]{:S(2)}, u32[]{:S(2)}) collective-permute-start(f32[384,128]{1,0:T(8,128)S(1)} %add.63.refs_0_), channel_id=1, source_target_pairs={{0,2},{2,0},{4,6},{6,4},{8,10},{10,8},{12,14},{14,12},{16,18},{18,... | collective-permute-start | bytes 589832 | tf_op jit(solution)/shard_map/ppermute | solution.py:277
  31.4 9.5 %collective-permute-start.3 = (f32[384,128]{1,0:T(8,128)S(1)}, f32[384,128]{1,0:T(8,128)S(1)}, u32[]{:S(2)}, u32[]{:S(2)}) collective-permute-start(f32[384,128]{1,0:T(8,128)S(1)} %add.63.refs_0_), channel_id=1, source_target_pairs={{0,30},{2,4},{4,2},{6,8},{8,6},{10,12},{12,10},{14,16},{16,14},{18... | collective-permute-start | bytes 589832 | tf_op jit(solution)/shard_map/ppermute | solution.py:277

commit v3 on v2

--- a/solution.py
+++ b/solution.py
@@ -11,7 +11,7 @@
 BF16 = jnp.bfloat16
 REACH = 3
 KERNEL_BYTES = 32 * 1024 * 1024
-LOADING_BYTES = 50 * 1024 * 1024
+LOADING_BYTES = 46 * 1024 * 1024
 
 
 def ring(peers, wrap):
@@ -41,51 +41,10 @@
     return place(below_part, 0) + place(centre_part, 1) + place(above_part, 2)
 
 
-def product_kernel(both_pairs, lines, chunks, start_ref, values_ref, potential_ref, *refs):
-    outs, (held, turned, total, means, levels, sems, level_sem) = refs[:-7], refs[-7:]
-    depth, size = held.shape[1:]
-    wide = size // REACH
-    block = wide // lines
-    start = start_ref[0]
-    level_copy = pltpu.make_async_copy(potential_ref.at[0], levels, level_sem)
-    level_copy.start()
-    copies = []
-    for c in range(chunks):
-        for a in range(REACH):
-            columns = pl.ds(pl.multiple_of(a * REACH * block + start * block, block), wide)
-            copies.append(
-                pltpu.make_async_copy(
-                    values_ref.at[0, 0, pl.ds(c * depth, depth), columns],
-                    held.at[c, :, pl.ds(a * wide, wide)],
-                    sems.at[c, a],
-                )
-            )
-            copies[-1].start()
-
-    def prepare(c):
-        for a in range(REACH):
-            copies[c * REACH + a].wait()
-        level = levels[:, c * depth : (c + 1) * depth]
-        turned[c % 2] = (held[c].T.astype(F32) * level).astype(BF16)
-
-    level_copy.wait()
-    prepare(0)
-    for c in range(chunks):
-        if c + 1 < chunks:
-            prepare(c + 1)
-        for n in range(0, size, 256):
-            for m in range(0, size, 768):
-                here = pl.ds(m, 768), pl.ds(n, 256)
-                part = jnp.dot(
-                    turned[c % 2, here[0], :], held[c, :, here[1]], preferred_element_type=F32
-                )
-                total[here] = part if c == 0 else total[here] + part
-
+def give(outs, both_pairs, odd, means, part, block):
     wanted = sorted({pair for lists in both_pairs for pairs in lists for pair in pairs})
     for n, (i, j) in enumerate(wanted):
-        rows, columns = pl.ds(i * block, block), pl.ds(j * block, block)
-        means[n] = 0.5 * (total[rows, columns] + total[columns, rows].T)
-    odd = start_ref[1] == 1
+        means[n] = 0.5 * (part(i, j) + part(j, i).T)
     for out, evens, odds in zip(outs, *both_pairs):
         for n, (even_pair, odd_pair) in enumerate(zip(evens, odds)):
             index = wanted.index(even_pair)
@@ -94,37 +53,112 @@
             out[n * block : (n + 1) * block, :] = means[index]
 
 
+def load_kernel(both_pairs, lines, start_ref, values_ref, potential_ref, *refs):
+    outs, (held, turned, ends, means, levels, sems, level_sem) = refs[:-7], refs[-7:]
+    wide = held.shape[2]
+    block = wide // lines
+    start = start_ref[0]
+    level_copy = pltpu.make_async_copy(potential_ref.at[0], levels, level_sem)
+    level_copy.start()
+    copies = {}
+    for a in (0, 2, 1):
+        columns = pl.ds(pl.multiple_of(a * REACH * block + start * block, block), wide)
+        copies[a] = pltpu.make_async_copy(
+            values_ref.at[0, 0, :, columns], held.at[a], sems.at[a]
+        )
+        copies[a].start()
+    level_copy.wait()
+
+    def prepare(a):
+        copies[a].wait()
+        turned[a * wide : (a + 1) * wide, :] = (held[a].T.astype(F32) * levels[...]).astype(BF16)
+
+    def multiply(a, b):
+        ends[a // 2, b // 2] = jnp.dot(
+            turned[a * wide : (a + 1) * wide, :], held[b], preferred_element_type=F32
+        )
+
+    prepare(0)
+    multiply(0, 0)
+    prepare(2)
+    multiply(0, 2)
+    multiply(2, 0)
+    prepare(1)
+    multiply(2, 2)
+
+    def part(i, j):
+        (a, r), (b, q) = divmod(i, lines), divmod(j, lines)
+        return ends[a // 2, b // 2, pl.ds(r * block, block), pl.ds(q * block, block)]
+
+    give(outs, both_pairs, start_ref[1] == 1, means, part, block)
+
+
+def rest_kernel(both_pairs, lines, start_ref, held, turned, *refs):
+    outs, (total, means) = refs[:-2], refs[-2:]
+    wide = held.shape[2]
+    block = wide // lines
+    for a, (low, high) in ((1, (0, 3)), (0, (1, 2)), (2, (1, 2))):
+        rows, columns = pl.ds(low * wide, (high - low) * wide), pl.ds(a * wide, wide)
+        total[rows, columns] = jnp.dot(turned[rows, :], held[a], preferred_element_type=F32)
+
+    def part(i, j):
+        return total[pl.ds(i * block, block), pl.ds(j * block, block)]
+
+    give(outs, both_pairs, start_ref[1] == 1, means, part, block)
+
+
 def local_products(values, potential, start, both_pairs, lines):
     points, width = values.shape[2:]
     block = width // (REACH * REACH)
-    size = block * lines * REACH
-    chunks = 1
+    wide = block * lines
+    size = wide * REACH
     vmem = pl.BlockSpec(memory_space=pltpu.VMEM)
-    counts = [len(pairs) for pairs in both_pairs[0]]
-    return pl.pallas_call(
-        functools.partial(product_kernel, both_pairs, lines, chunks),
-        out_shape=[jax.ShapeDtypeStruct((n * block, block), F32) for n in counts],
-        in_specs=[
-            pl.BlockSpec(memory_space=pltpu.SMEM),
-            pl.BlockSpec(memory_space=pltpu.HBM),
-            pl.BlockSpec(memory_space=pltpu.HBM),
+    smem = pl.BlockSpec(memory_space=pltpu.SMEM)
+    hbm = pl.BlockSpec(memory_space=pltpu.HBM)
+    first, rest = ([lists[:3] for lists in both_pairs], [lists[3:] for lists in both_pairs])
+
+    def shapes(lists):
+        return [jax.ShapeDtypeStruct((len(pairs) * block, block), F32) for pairs in lists[0]]
+
+    def means(lists):
+        return pltpu.VMEM((len({p for ls in lists for ps in ls for p in ps}), block, block), F32)
+
+    params = pltpu.CompilerParams(vmem_limit_bytes=LOADING_BYTES)
+    *ends, held, turned = pl.pallas_call(
+        functools.partial(load_kernel, first, lines),
+        out_shape=shapes(first)
+        + [
+            jax.ShapeDtypeStruct((REACH, points, wide), BF16),
+            jax.ShapeDtypeStruct((size, points), BF16),
         ],
-        out_specs=[vmem] * len(counts),
+        in_specs=[smem, hbm, hbm],
+        out_specs=[vmem] * (len(first[0]) + 2),
         scratch_shapes=[
-            pltpu.VMEM((chunks, points // chunks, size), BF16),
-            pltpu.VMEM((2, size, points // chunks), BF16),
-            pltpu.VMEM((size, size), F32),
-            pltpu.VMEM((REACH * REACH * lines * lines, block, block), F32),
+            pltpu.VMEM((2, 2, wide, wide), F32),
+            means(first),
             pltpu.VMEM((1, points), F32),
-            pltpu.SemaphoreType.DMA((chunks, REACH)),
+            pltpu.SemaphoreType.DMA((REACH,)),
             pltpu.SemaphoreType.DMA,
         ],
-        compiler_params=pltpu.CompilerParams(vmem_limit_bytes=LOADING_BYTES),
+        compiler_params=params,
         cost_estimate=pl.CostEstimate(
-            flops=2 * points * size * size, bytes_accessed=2 * points * size, transcendentals=0
+            flops=8 * points * wide * wide, bytes_accessed=2 * points * size, transcendentals=0
         ),
-        name="products",
+        name="ends",
     )(start, values, potential)
+    others = pl.pallas_call(
+        functools.partial(rest_kernel, rest, lines),
+        out_shape=shapes(rest),
+        in_specs=[smem, vmem, vmem],
+        out_specs=[vmem] * len(rest[0]),
+        scratch_shapes=[pltpu.VMEM((size, size), F32), means(rest)],
+        compiler_params=params,
+        cost_estimate=pl.CostEstimate(
+            flops=10 * points * wide * wide, bytes_accessed=0, transcendentals=0
+        ),
+        name="others",
+    )(start, held, turned)
+    return [*ends, *others]
 
 
 def sign_kernel(slots, block, own_tile, place, meta_ref, *refs):
@@ -294,14 +328,14 @@
         return (
             within(2 * odd),
             within(2 - 2 * odd),
+            [(r, 2 * lines + q) for r in range(lines) for q in range(lines)],
             across(odd, not odd),
             across(1 - odd, odd),
             within(1),
             across(odd, odd) + across(1 - odd, not odd),
-            [(r, 2 * lines + q) for r in range(lines) for q in range(lines)],
         )
 
-    own_to_far, own_to_near, side_to_far, side_to_near, own, side, outer = local_products(
+    own_to_far, own_to_near, outer, side_to_far, side_to_near, own, side = local_products(
         basis_values, potential, start, (pairs_of(0), pairs_of(1)), lines
     )
     outer_parts = [outer] + line_parts(outer)

time: 47.6 us -> 48.7 us (1.023)
  Pallas kernels: 11.8 us -> 12.9 us
    pallas_call x1 -> x2, Pallas kernels: 5.39 us -> 6.5 us  [the longest x1 4.19 us: local_products(): pl.pallas_call(functools.partial(load_kernel, first, lines), out_shape=sh...]
where the time goes in v3:
time: 48.7 us; the launch traced here: 48.5 us
  starting transfers between devices  20.3 us (42%)
  Pallas kernels  12.9 us (26%)
  waiting for transfers between devices  12.8 us (26%)
  local copies, waits for them, and re-layouts  1.43 us (3%)
  other arithmetic  0.97 us (2%)
    ppermute x11, starting transfers between devices, sent(): return lax.ppermute(part, axis, pairs)  20.3 us
    ppermute x11, waiting for transfers between devices, sent(): return lax.ppermute(part, axis, pairs)  12.8 us
    pallas_call x1, Pallas kernels, sign_columns(): pl.pallas_call(functools.partial(sign_kernel, slots, block, own_tile, pla...  6.43 us
    pallas_call x1, Pallas kernels, local_products(): pl.pallas_call(functools.partial(load_kernel, first, lines), out_shape=sh...  4.19 us
    pallas_call x1, Pallas kernels, local_products(): pl.pallas_call(functools.partial(rest_kernel, rest, lines), out_shape=sha...  2.31 us
  transfers between devices with their start and end apart: 11, of which 5 were waited for; matrix products, arithmetic and copies ran while one was open for 3% of the time, Pallas kernels for 0%

profile of v3, /device:TPU:0, one launch (start us, length us, event | category | flops | bytes accessed | tf_op | source)
XLA Modules:
  0.0 48.5 jit_solution(3549615565826121732)
XLA Ops:
  0.0 0.1 pad_add_fusion.start_ref
  0.1 0.0 copy-start
  0.1 0.7 %copy-done = f32[1,1,2048]{2,1,0:T(1,128)S(1)} copy-done((f32[1,1,2048]{2,1,0:T(1,128)S(1)}, f32[1,1,2048]{2,1,0:T(1,128)}, u32[]{:S(2)}) %copy-start) | copy-done | bytes 8216
  0.8 4.2 %ends.1 = (f32[384,128]{1,0:T(8,128)S(1)}, f32[384,128]{1,0:T(8,128)S(1)}, f32[512,128]{1,0:T(8,128)S(1)}, bf16[3,2048,256]{2,1,0:T(8,128)(2,1)S(1)}, bf16[768,2048]{1,0:T(8,128)(2,1)S(1)}) custom-call(s32[2]{0:T(128)S(1)} %pad_add_fusion.start_ref, bf16[1,1,2048,1152]{3,2,1,0:T(8,128)(2,1)} %values_ref.1, f32[1,1,2048]{2,1,0:T(1,128)S(1)} %copy-done), custom_call_target="tpu_custom_call" | custom-call | flops 1073741824 | bytes 3145728 | tf_op jit(solution)/shard_map/ends/pallas_call | solution.py:127
  5.0 2.3 %others.1 = (f32[256,128]{1,0:T(8,128)S(1)}, f32[256,128]{1,0:T(8,128)S(1)}, f32[384,128]{1,0:T(8,128)S(1)}, f32[512,128]{1,0:T(8,128)S(1)}) custom-call(s32[2]{0:T(128)S(1)} %pad_add_fusion.start_ref, bf16[3,2048,256]{2,1,0:T(8,128)(2,1)S(1)} %get-tuple-element.14.held, bf16[768,2048]{1,0:T(8,128)(2,1)S(1)} %get-tuple-element.15.turned), custom_call_target="tpu_custom_call" | custom-call | flops 1342177280 | tf_op jit(solution)/shard_map/others/pallas_call | solution.py:149
  7.3 0.0 copy-start.1
  7.3 5.5 %collective-permute-start.5 = (f32[256,128]{1,0:T(8,128)S(1)}, f32[256,128]{1,0:T(8,128)S(1)}, u32[]{:S(2)}, u32[]{:S(2)}) collective-permute-start(f32[256,128]{1,0:T(8,128)S(1)} %get-tuple-element.20), channel_id=1, source_target_pairs={{0,30},{2,4},{4,2},{6,8},{8,6},{10,12},{12,10},{14,16},{16,14},{18... | collective-permute-start | bytes 393224 | tf_op jit(solution)/shard_map/ppermute | solution.py:311
  12.8 0.0 collective-permute-start.6
  12.8 0.7 %collective-permute-start = (f32[384,128]{1,0:T(8,128)S(1)}, f32[384,128]{1,0:T(8,128)S(1)}, u32[]{:S(2)}, u32[]{:S(2)}) collective-permute-start(f32[384,128]{1,0:T(8,128)S(1)} %get-tuple-element.17), channel_id=1, source_target_pairs={{0,30},{2,4},{4,2},{6,8},{8,6},{10,12},{12,10},{14,16},{16,14},{18... | collective-permute-start | bytes 589832 | tf_op jit(solution)/shard_map/ppermute | solution.py:311
  13.6 0.0 collective-permute-start.1
  13.6 1.9 %collective-permute-done.5 = f32[256,128]{1,0:T(8,128)S(1)} collective-permute-done((f32[256,128]{1,0:T(8,128)S(1)}, f32[256,128]{1,0:T(8,128)S(1)}, u32[]{:S(2)}, u32[]{:S(2)}) %collective-permute-start.5) | collective-permute-done | bytes 131104 | tf_op jit(solution)/shard_map/ppermute | solution.py:311
  15.5 0.0 collective-permute-done.6
  15.5 2.1 %collective-permute-start.7 = (f32[512,128]{1,0:T(8,128)S(1)}, f32[512,128]{1,0:T(8,128)S(1)}, u32[]{:S(2)}, u32[]{:S(2)}) collective-permute-start(f32[512,128]{1,0:T(8,128)S(1)} %maximum_add_fusion), channel_id=1, source_target_pairs={{0,1},{1,0},{2,3},{3,2},{4,5},{5,4},{6,7},{7,6},{8,9},{9,8},{10,11... | collective-permute-start | bytes 786440 | tf_op jit(solution)/shard_map/ppermute | solution.py:311
  17.6 0.1 collective-permute-start.10
  17.6 3.1 %collective-permute-done = f32[384,128]{1,0:T(8,128)S(1)} collective-permute-done((f32[384,128]{1,0:T(8,128)S(1)}, f32[384,128]{1,0:T(8,128)S(1)}, u32[]{:S(2)}, u32[]{:S(2)}) %collective-permute-start) | collective-permute-done | bytes 196640 | tf_op jit(solution)/shard_map/ppermute | solution.py:311
  20.7 0.0 collective-permute-done.1
  20.7 1.6 %collective-permute-start.2 = (f32[384,128]{1,0:T(8,128)S(1)}, f32[384,128]{1,0:T(8,128)S(1)}, u32[]{:S(2)}, u32[]{:S(2)}) collective-permute-start(f32[384,128]{1,0:T(8,128)S(1)} %add_add_fusion), channel_id=1, source_target_pairs={{0,1},{1,0},{2,3},{3,2},{4,5},{5,4},{6,7},{7,6},{8,9},{9,8},{10,11... | collective-permute-start | bytes 589832 | tf_op jit(solution)/shard_map/ppermute | solution.py:311
  22.3 2.4 %collective-permute-done.7 = f32[512,128]{1,0:T(8,128)S(1)} collective-permute-done((f32[512,128]{1,0:T(8,128)S(1)}, f32[512,128]{1,0:T(8,128)S(1)}, u32[]{:S(2)}, u32[]{:S(2)}) %collective-permute-start.7) | collective-permute-done | bytes 262176 | tf_op jit(solution)/shard_map/ppermute | solution.py:311
  24.8 0.1 collective-permute-start.9
  24.9 4.0 %collective-permute-start.8 = (f32[256,128]{1,0:T(8,128)S(1)}, f32[256,128]{1,0:T(8,128)S(1)}, u32[]{:S(2)}, u32[]{:S(2)}) collective-permute-start(f32[256,128]{1,0:T(8,128)S(1)} %get-tuple-element.24), channel_id=1, source_target_pairs={{0,30},{2,4},{4,2},{6,8},{8,6},{10,12},{12,10},{14,16},{16,14},{18... | collective-permute-start | bytes 393224 | tf_op jit(solution)/shard_map/ppermute | solution.py:311
  28.9 3.5 %collective-permute-done.2 = f32[384,128]{1,0:T(8,128)S(1)} collective-permute-done((f32[384,128]{1,0:T(8,128)S(1)}, f32[384,128]{1,0:T(8,128)S(1)}, u32[]{:S(2)}, u32[]{:S(2)}) %collective-permute-start.2) | collective-permute-done | bytes 196640 | tf_op jit(solution)/shard_map/ppermute | solution.py:311
  32.5 0.1 collective-permute-start.4
  32.6 6.1 %collective-permute-start.3 = (f32[384,128]{1,0:T(8,128)S(1)}, f32[384,128]{1,0:T(8,128)S(1)}, u32[]{:S(2)}, u32[]{:S(2)}) collective-permute-start(f32[384,128]{1,0:T(8,128)S(1)} %add.63.refs_0_), channel_id=1, source_target_pairs={{0,30},{2,4},{4,2},{6,8},{8,6},{10,12},{12,10},{14,16},{16,14},{18... | collective-permute-start | bytes 589832 | tf_op jit(solution)/shard_map/ppermute | solution.py:311
  38.7 0.0 copy-done.1
  38.7 0.7 %bitcast_select_fusion = (s32[6]{0:T(128)S(1)}, s32[]{:T(128)}) fusion(s32[1,1,6]{2,1,0:T(1,128)S(1)} %copy-done.1, s32[]{:T(128)} %axis_index.22), kind=kLoop, calls=%fused_computation.6 | loop fusion | flops 119 | bytes 56 | tf_op jit(solution)/shard_map/jit(_where)/select_n | solution.py:368
  39.4 0.1 convert_reduce_fusion
  39.5 0.7 %concatenate.6.meta_ref = s32[15]{0:T(128)S(1)} concatenate(s32[1]{0:T(128)} %bitcast.1, s32[1]{0:T(128)} %bitcast.2, s32[6]{0:T(128)S(1)} %convert_reduce_fusion, s32[6]{0:T(128)S(1)} %get-tuple-element.25, s32[1]{0:T(128)} %bitcast.6), dimensions={0} | concatenate | bytes 120 | tf_op jit(solution)/shard_map/concatenate | solution.py:371
  40.2 0.0 collective-permute-done.10.refs_7_
  40.2 0.0 collective-permute-done.9.refs_5_
  40.2 0.0 collective-permute-done.8.refs_4_
  40.2 0.0 collective-permute-done.4.refs_2_
  40.2 1.8 %collective-permute-done.3.refs_1_ = f32[384,128]{1,0:T(8,128)S(1)} collective-permute-done((f32[384,128]{1,0:T(8,128)S(1)}, f32[384,128]{1,0:T(8,128)S(1)}, u32[]{:S(2)}, u32[]{:S(2)}) %collective-permute-start.3) | collective-permute-done | bytes 196640 | tf_op jit(solution)/shard_map/ppermute | solution.py:311
  42.1 6.4 %sign.14 = f32[768,128]{1,0:T(8,128)} custom-call(s32[15]{0:T(128)S(1)} %concatenate.6.meta_ref, f32[384,128]{1,0:T(8,128)S(1)} %add.63.refs_0_, f32[384,128]{1,0:T(8,128)S(1)} %collective-permute-done.3.refs_1_, f32[384,128]{1,0:T(8,128)S(1)} %collective-permute-done.4.refs_2_, f32[512,128]{1,0:T(8,128)S(1)} %add.65.refs_3_, ...), custom_call_target="tpu_custom_call" | custom-call | flops 3623878656 | bytes 2359296 | tf_op jit(solution)/shard_map/sign/pallas_call | solution.py:276
  (5 shorter events, 0.1 us)
Async XLA Ops:
  0.1 0.7 %copy-start = (f32[1,1,2048]{2,1,0:T(1,128)S(1)}, f32[1,1,2048]{2,1,0:T(1,128)}, u32[]{:S(2)}) copy-start(f32[1,1,2048]{2,1,0:T(1,128)} %potential_ref.1) | copy-start | bytes 24580
  7.3 31.4 %copy-start.1 = (s32[1,1,6]{2,1,0:T(1,128)S(1)}, s32[1,1,6]{2,1,0:T(1,128)}, u32[]{:S(2)}) copy-start(s32[1,1,6]{2,1,0:T(1,128)} %param.5) | copy-start | bytes 76
  7.3 8.2 %collective-permute-start.5 = (f32[256,128]{1,0:T(8,128)S(1)}, f32[256,128]{1,0:T(8,128)S(1)}, u32[]{:S(2)}, u32[]{:S(2)}) collective-permute-start(f32[256,128]{1,0:T(8,128)S(1)} %get-tuple-element.20), channel_id=1, source_target_pairs={{0,30},{2,4},{4,2},{6,8},{8,6},{10,12},{12,10},{14,16},{16,14},{18... | collective-permute-start | bytes 393224 | tf_op jit(solution)/shard_map/ppermute | solution.py:311
  12.8 2.7 %collective-permute-start.6 = (f32[256,128]{1,0:T(8,128)S(1)}, f32[256,128]{1,0:T(8,128)S(1)}, u32[]{:S(2)}, u32[]{:S(2)}) collective-permute-start(f32[256,128]{1,0:T(8,128)S(1)} %get-tuple-element.21), channel_id=1, source_target_pairs={{0,2},{2,0},{4,6},{6,4},{8,10},{10,8},{12,14},{14,12},{16,18},{18,... | collective-permute-start | bytes 393224 | tf_op jit(solution)/shard_map/ppermute | solution.py:311
  12.8 7.9 %collective-permute-start = (f32[384,128]{1,0:T(8,128)S(1)}, f32[384,128]{1,0:T(8,128)S(1)}, u32[]{:S(2)}, u32[]{:S(2)}) collective-permute-start(f32[384,128]{1,0:T(8,128)S(1)} %get-tuple-element.17), channel_id=1, source_target_pairs={{0,30},{2,4},{4,2},{6,8},{8,6},{10,12},{12,10},{14,16},{16,14},{18... | collective-permute-start | bytes 589832 | tf_op jit(solution)/shard_map/ppermute | solution.py:311
  13.6 7.1 %collective-permute-start.1 = (f32[384,128]{1,0:T(8,128)S(1)}, f32[384,128]{1,0:T(8,128)S(1)}, u32[]{:S(2)}, u32[]{:S(2)}) collective-permute-start(f32[384,128]{1,0:T(8,128)S(1)} %get-tuple-element.18), channel_id=1, source_target_pairs={{0,2},{2,0},{4,6},{6,4},{8,10},{10,8},{12,14},{14,12},{16,18},{18,... | collective-permute-start | bytes 589832 | tf_op jit(solution)/shard_map/ppermute | solution.py:311
  15.5 9.2 %collective-permute-start.7 = (f32[512,128]{1,0:T(8,128)S(1)}, f32[512,128]{1,0:T(8,128)S(1)}, u32[]{:S(2)}, u32[]{:S(2)}) collective-permute-start(f32[512,128]{1,0:T(8,128)S(1)} %maximum_add_fusion), channel_id=1, source_target_pairs={{0,1},{1,0},{2,3},{3,2},{4,5},{5,4},{6,7},{7,6},{8,9},{9,8},{10,11... | collective-permute-start | bytes 786440 | tf_op jit(solution)/shard_map/ppermute | solution.py:311
  17.6 22.6 %collective-permute-start.10 = (f32[512,128]{1,0:T(8,128)S(1)}, f32[512,128]{1,0:T(8,128)S(1)}, u32[]{:S(2)}, u32[]{:S(2)}) collective-permute-start(f32[512,128]{1,0:T(8,128)S(1)} %get-tuple-element.22.refs_6_), channel_id=1, source_target_pairs={{0,1},{1,0},{2,3},{3,2},{4,5},{5,4},{6,7},{7,6},{8,9},{9,8},{10,11... | collective-permute-start | bytes 786440 | tf_op jit(solution)/shard_map/ppermute | solution.py:311
  20.7 11.7 %collective-permute-start.2 = (f32[384,128]{1,0:T(8,128)S(1)}, f32[384,128]{1,0:T(8,128)S(1)}, u32[]{:S(2)}, u32[]{:S(2)}) collective-permute-start(f32[384,128]{1,0:T(8,128)S(1)} %add_add_fusion), channel_id=1, source_target_pairs={{0,1},{1,0},{2,3},{3,2},{4,5},{5,4},{6,7},{7,6},{8,9},{9,8},{10,11... | collective-permute-start | bytes 589832 | tf_op jit(solution)/shard_map/ppermute | solution.py:311
  24.8 15.4 %collective-permute-start.9 = (f32[256,128]{1,0:T(8,128)S(1)}, f32[256,128]{1,0:T(8,128)S(1)}, u32[]{:S(2)}, u32[]{:S(2)}) collective-permute-start(f32[256,128]{1,0:T(8,128)S(1)} %get-tuple-element.23), channel_id=1, source_target_pairs={{0,2},{2,0},{4,6},{6,4},{8,10},{10,8},{12,14},{14,12},{16,18},{18,... | collective-permute-start | bytes 393224 | tf_op jit(solution)/shard_map/ppermute | solution.py:311
  24.9 15.3 %collective-permute-start.8 = (f32[256,128]{1,0:T(8,128)S(1)}, f32[256,128]{1,0:T(8,128)S(1)}, u32[]{:S(2)}, u32[]{:S(2)}) collective-permute-start(f32[256,128]{1,0:T(8,128)S(1)} %get-tuple-element.24), channel_id=1, source_target_pairs={{0,30},{2,4},{4,2},{6,8},{8,6},{10,12},{12,10},{14,16},{16,14},{18... | collective-permute-start | bytes 393224 | tf_op jit(solution)/shard_map/ppermute | solution.py:311
  32.5 7.7 %collective-permute-start.4 = (f32[384,128]{1,0:T(8,128)S(1)}, f32[384,128]{1,0:T(8,128)S(1)}, u32[]{:S(2)}, u32[]{:S(2)}) collective-permute-start(f32[384,128]{1,0:T(8,128)S(1)} %add.63.refs_0_), channel_id=1, source_target_pairs={{0,2},{2,0},{4,6},{6,4},{8,10},{10,8},{12,14},{14,12},{16,18},{18,... | collective-permute-start | bytes 589832 | tf_op jit(solution)/shard_map/ppermute | solution.py:311
  32.6 9.5 %collective-permute-start.3 = (f32[384,128]{1,0:T(8,128)S(1)}, f32[384,128]{1,0:T(8,128)S(1)}, u32[]{:S(2)}, u32[]{:S(2)}) collective-permute-start(f32[384,128]{1,0:T(8,128)S(1)} %add.63.refs_0_), channel_id=1, source_target_pairs={{0,30},{2,4},{4,2},{6,8},{8,6},{10,12},{12,10},{14,16},{16,14},{18... | collective-permute-start | bytes 589832 | tf_op jit(solution)/shard_map/ppermute | solution.py:311

commit v4 on v3

--- a/solution.py
+++ b/solution.py
@@ -61,30 +61,29 @@
     level_copy = pltpu.make_async_copy(potential_ref.at[0], levels, level_sem)
     level_copy.start()
     copies = {}
-    for a in (0, 2, 1):
+    for a in (0, 2):
         columns = pl.ds(pl.multiple_of(a * REACH * block + start * block, block), wide)
         copies[a] = pltpu.make_async_copy(
-            values_ref.at[0, 0, :, columns], held.at[a], sems.at[a]
+            values_ref.at[0, 0, :, columns], held.at[a // 2], sems.at[a // 2]
         )
         copies[a].start()
     level_copy.wait()
 
     def prepare(a):
-        copies[a].wait()
+        copies[2 * a].wait()
         turned[a * wide : (a + 1) * wide, :] = (held[a].T.astype(F32) * levels[...]).astype(BF16)
 
     def multiply(a, b):
-        ends[a // 2, b // 2] = jnp.dot(
+        ends[a, b] = jnp.dot(
             turned[a * wide : (a + 1) * wide, :], held[b], preferred_element_type=F32
         )
 
     prepare(0)
     multiply(0, 0)
-    prepare(2)
-    multiply(0, 2)
-    multiply(2, 0)
     prepare(1)
-    multiply(2, 2)
+    multiply(0, 1)
+    multiply(1, 0)
+    multiply(1, 1)
 
     def part(i, j):
         (a, r), (b, q) = divmod(i, lines), divmod(j, lines)
@@ -93,13 +92,26 @@
     give(outs, both_pairs, start_ref[1] == 1, means, part, block)
 
 
-def rest_kernel(both_pairs, lines, start_ref, held, turned, *refs):
-    outs, (total, means) = refs[:-2], refs[-2:]
+def rest_kernel(both_pairs, lines, start_ref, values_ref, potential_ref, held, turned, *refs):
+    outs, (total, means, middle, centre, levels, sems) = refs[:-6], refs[-6:]
     wide = held.shape[2]
     block = wide // lines
-    for a, (low, high) in ((1, (0, 3)), (0, (1, 2)), (2, (1, 2))):
-        rows, columns = pl.ds(low * wide, (high - low) * wide), pl.ds(a * wide, wide)
-        total[rows, columns] = jnp.dot(turned[rows, :], held[a], preferred_element_type=F32)
+    columns = pl.ds(pl.multiple_of(REACH * block + start_ref[0] * block, block), wide)
+    copy = pltpu.make_async_copy(values_ref.at[0, 0, :, columns], middle, sems.at[0])
+    copy.start()
+    level_copy = pltpu.make_async_copy(potential_ref.at[0], levels, sems.at[1])
+    level_copy.start()
+    level_copy.wait()
+    copy.wait()
+    centre[...] = (middle[...].T.astype(F32) * levels[...]).astype(BF16)
+    inner = pl.ds(wide, wide)
+    for a in range(2):
+        outer = pl.ds(2 * a * wide, wide)
+        total[outer, inner] = jnp.dot(
+            turned[a * wide : (a + 1) * wide, :], middle[...], preferred_element_type=F32
+        )
+        total[inner, outer] = jnp.dot(centre[...], held[a], preferred_element_type=F32)
+    total[inner, inner] = jnp.dot(centre[...], middle[...], preferred_element_type=F32)
 
     def part(i, j):
         return total[pl.ds(i * block, block), pl.ds(j * block, block)]
@@ -128,8 +140,8 @@
         functools.partial(load_kernel, first, lines),
         out_shape=shapes(first)
         + [
-            jax.ShapeDtypeStruct((REACH, points, wide), BF16),
-            jax.ShapeDtypeStruct((size, points), BF16),
+            jax.ShapeDtypeStruct((2, points, wide), BF16),
+            jax.ShapeDtypeStruct((2 * wide, points), BF16),
         ],
         in_specs=[smem, hbm, hbm],
         out_specs=[vmem] * (len(first[0]) + 2),
@@ -137,7 +149,7 @@
             pltpu.VMEM((2, 2, wide, wide), F32),
             means(first),
             pltpu.VMEM((1, points), F32),
-            pltpu.SemaphoreType.DMA((REACH,)),
+            pltpu.SemaphoreType.DMA((2,)),
             pltpu.SemaphoreType.DMA,
         ],
         compiler_params=params,
@@ -149,15 +161,22 @@
     others = pl.pallas_call(
         functools.partial(rest_kernel, rest, lines),
         out_shape=shapes(rest),
-        in_specs=[smem, vmem, vmem],
+        in_specs=[smem, hbm, hbm, vmem, vmem],
         out_specs=[vmem] * len(rest[0]),
-        scratch_shapes=[pltpu.VMEM((size, size), F32), means(rest)],
+        scratch_shapes=[
+            pltpu.VMEM((size, size), F32),
+            means(rest),
+            pltpu.VMEM((points, wide), BF16),
+            pltpu.VMEM((wide, points), BF16),
+            pltpu.VMEM((1, points), F32),
+            pltpu.SemaphoreType.DMA((2,)),
+        ],
         compiler_params=params,
         cost_estimate=pl.CostEstimate(
             flops=10 * points * wide * wide, bytes_accessed=0, transcendentals=0
         ),
         name="others",
-    )(start, held, turned)
+    )(start, values, potential, held, turned)
     return [*ends, *others]
 
 

time: 48.7 us -> 49.7 us (1.021)
  Pallas kernels: 12.9 us -> 13.9 us
    pallas_call x1, Pallas kernels: 2.31 us -> 3.55 us  [local_products(): pl.pallas_call(functools.partial(rest_kernel, rest, lines), out_shape=sha...]
where the time goes in v4:
time: 49.7 us; the launch traced here: 49.5 us
  starting transfers between devices  20.3 us (41%)
  Pallas kernels  13.9 us (28%)
  waiting for transfers between devices  12.8 us (26%)
  local copies, waits for them, and re-layouts  1.43 us (3%)
  other arithmetic  0.95 us (2%)
    ppermute x11, starting transfers between devices, sent(): return lax.ppermute(part, axis, pairs)  20.3 us
    ppermute x11, waiting for transfers between devices, sent(): return lax.ppermute(part, axis, pairs)  12.8 us
    pallas_call x1, Pallas kernels, sign_columns(): pl.pallas_call(functools.partial(sign_kernel, slots, block, own_tile, pla...  6.44 us
    pallas_call x1, Pallas kernels, local_products(): pl.pallas_call(functools.partial(load_kernel, first, lines), out_shape=sh...  3.95 us
    pallas_call x1, Pallas kernels, local_products(): pl.pallas_call(functools.partial(rest_kernel, rest, lines), out_shape=sha...  3.55 us
  transfers between devices with their start and end apart: 11, of which 5 were waited for; matrix products, arithmetic and copies ran while one was open for 3% of the time, Pallas kernels for 0%

profile of v4, /device:TPU:0, one launch (start us, length us, event | category | flops | bytes accessed | tf_op | source)
XLA Modules:
  0.0 49.5 jit_solution(12605779461999294699)
XLA Ops:
  0.0 0.1 pad_add_fusion.start_ref
  0.1 0.0 copy-start
  0.1 0.7 %copy-done = f32[1,1,2048]{2,1,0:T(1,128)S(1)} copy-done((f32[1,1,2048]{2,1,0:T(1,128)S(1)}, f32[1,1,2048]{2,1,0:T(1,128)}, u32[]{:S(2)}) %copy-start) | copy-done | bytes 8216
  0.8 4.0 %ends.1 = (f32[384,128]{1,0:T(8,128)S(1)}, f32[384,128]{1,0:T(8,128)S(1)}, f32[512,128]{1,0:T(8,128)S(1)}, bf16[2,2048,256]{2,1,0:T(8,128)(2,1)S(1)}, bf16[512,2048]{1,0:T(8,128)(2,1)S(1)}) custom-call(s32[2]{0:T(128)S(1)} %pad_add_fusion.start_ref, bf16[1,1,2048,1152]{3,2,1,0:T(8,128)(2,1)} %values_ref.3, f32[1,1,2048]{2,1,0:T(1,128)S(1)} %copy-done), custom_call_target="tpu_custom_call" | custom-call | flops 1073741824 | bytes 3145728 | tf_op jit(solution)/shard_map/ends/pallas_call | solution.py:139
  4.7 3.5 %others.1 = (f32[256,128]{1,0:T(8,128)S(1)}, f32[256,128]{1,0:T(8,128)S(1)}, f32[384,128]{1,0:T(8,128)S(1)}, f32[512,128]{1,0:T(8,128)S(1)}) custom-call(s32[2]{0:T(128)S(1)} %pad_add_fusion.start_ref, bf16[1,1,2048,1152]{3,2,1,0:T(8,128)(2,1)} %values_ref.3, f32[1,1,2048]{2,1,0:T(1,128)S(1)} %copy-done, bf16[2,2048,256]{2,1,0:T(8,128)(2,1)S(1)} %get-tuple-element.14.held, ...), custom_call_target="tpu_custom_call" | custom-call | flops 1342177280 | tf_op jit(solution)/shard_map/others/pallas_call | solution.py:161
  8.3 0.0 copy-start.1
  8.3 5.5 %collective-permute-start.5 = (f32[256,128]{1,0:T(8,128)S(1)}, f32[256,128]{1,0:T(8,128)S(1)}, u32[]{:S(2)}, u32[]{:S(2)}) collective-permute-start(f32[256,128]{1,0:T(8,128)S(1)} %get-tuple-element.20), channel_id=1, source_target_pairs={{0,30},{2,4},{4,2},{6,8},{8,6},{10,12},{12,10},{14,16},{16,14},{18... | collective-permute-start | bytes 393224 | tf_op jit(solution)/shard_map/ppermute | solution.py:330
  13.8 0.0 collective-permute-start.6
  13.8 0.7 %collective-permute-start = (f32[384,128]{1,0:T(8,128)S(1)}, f32[384,128]{1,0:T(8,128)S(1)}, u32[]{:S(2)}, u32[]{:S(2)}) collective-permute-start(f32[384,128]{1,0:T(8,128)S(1)} %get-tuple-element.17), channel_id=1, source_target_pairs={{0,30},{2,4},{4,2},{6,8},{8,6},{10,12},{12,10},{14,16},{16,14},{18... | collective-permute-start | bytes 589832 | tf_op jit(solution)/shard_map/ppermute | solution.py:330
  14.6 0.0 collective-permute-start.1
  14.6 1.9 %collective-permute-done.5 = f32[256,128]{1,0:T(8,128)S(1)} collective-permute-done((f32[256,128]{1,0:T(8,128)S(1)}, f32[256,128]{1,0:T(8,128)S(1)}, u32[]{:S(2)}, u32[]{:S(2)}) %collective-permute-start.5) | collective-permute-done | bytes 131104 | tf_op jit(solution)/shard_map/ppermute | solution.py:330
  16.5 0.0 collective-permute-done.6
  16.5 2.1 %collective-permute-start.7 = (f32[512,128]{1,0:T(8,128)S(1)}, f32[512,128]{1,0:T(8,128)S(1)}, u32[]{:S(2)}, u32[]{:S(2)}) collective-permute-start(f32[512,128]{1,0:T(8,128)S(1)} %maximum_add_fusion), channel_id=1, source_target_pairs={{0,1},{1,0},{2,3},{3,2},{4,5},{5,4},{6,7},{7,6},{8,9},{9,8},{10,11... | collective-permute-start | bytes 786440 | tf_op jit(solution)/shard_map/ppermute | solution.py:330
  18.5 0.1 collective-permute-start.10
  18.6 3.1 %collective-permute-done = f32[384,128]{1,0:T(8,128)S(1)} collective-permute-done((f32[384,128]{1,0:T(8,128)S(1)}, f32[384,128]{1,0:T(8,128)S(1)}, u32[]{:S(2)}, u32[]{:S(2)}) %collective-permute-start) | collective-permute-done | bytes 196640 | tf_op jit(solution)/shard_map/ppermute | solution.py:330
  21.7 0.0 collective-permute-done.1
  21.7 1.6 %collective-permute-start.2 = (f32[384,128]{1,0:T(8,128)S(1)}, f32[384,128]{1,0:T(8,128)S(1)}, u32[]{:S(2)}, u32[]{:S(2)}) collective-permute-start(f32[384,128]{1,0:T(8,128)S(1)} %add_add_fusion), channel_id=1, source_target_pairs={{0,1},{1,0},{2,3},{3,2},{4,5},{5,4},{6,7},{7,6},{8,9},{9,8},{10,11... | collective-permute-start | bytes 589832 | tf_op jit(solution)/shard_map/ppermute | solution.py:330
  23.3 2.4 %collective-permute-done.7 = f32[512,128]{1,0:T(8,128)S(1)} collective-permute-done((f32[512,128]{1,0:T(8,128)S(1)}, f32[512,128]{1,0:T(8,128)S(1)}, u32[]{:S(2)}, u32[]{:S(2)}) %collective-permute-start.7) | collective-permute-done | bytes 262176 | tf_op jit(solution)/shard_map/ppermute | solution.py:330
  25.8 0.1 collective-permute-start.9
  25.9 4.0 %collective-permute-start.8 = (f32[256,128]{1,0:T(8,128)S(1)}, f32[256,128]{1,0:T(8,128)S(1)}, u32[]{:S(2)}, u32[]{:S(2)}) collective-permute-start(f32[256,128]{1,0:T(8,128)S(1)} %get-tuple-element.24), channel_id=1, source_target_pairs={{0,30},{2,4},{4,2},{6,8},{8,6},{10,12},{12,10},{14,16},{16,14},{18... | collective-permute-start | bytes 393224 | tf_op jit(solution)/shard_map/ppermute | solution.py:330
  29.9 3.5 %collective-permute-done.2 = f32[384,128]{1,0:T(8,128)S(1)} collective-permute-done((f32[384,128]{1,0:T(8,128)S(1)}, f32[384,128]{1,0:T(8,128)S(1)}, u32[]{:S(2)}, u32[]{:S(2)}) %collective-permute-start.2) | collective-permute-done | bytes 196640 | tf_op jit(solution)/shard_map/ppermute | solution.py:330
  33.5 0.1 collective-permute-start.4
  33.5 6.1 %collective-permute-start.3 = (f32[384,128]{1,0:T(8,128)S(1)}, f32[384,128]{1,0:T(8,128)S(1)}, u32[]{:S(2)}, u32[]{:S(2)}) collective-permute-start(f32[384,128]{1,0:T(8,128)S(1)} %add.63.refs_0_), channel_id=1, source_target_pairs={{0,30},{2,4},{4,2},{6,8},{8,6},{10,12},{12,10},{14,16},{16,14},{18... | collective-permute-start | bytes 589832 | tf_op jit(solution)/shard_map/ppermute | solution.py:330
  39.7 0.0 copy-done.1
  39.7 0.7 %bitcast_select_fusion = (s32[6]{0:T(128)S(1)}, s32[]{:T(128)}) fusion(s32[1,1,6]{2,1,0:T(1,128)S(1)} %copy-done.1, s32[]{:T(128)} %axis_index.22), kind=kLoop, calls=%fused_computation.6 | loop fusion | flops 119 | bytes 56 | tf_op jit(solution)/shard_map/jit(_where)/select_n | solution.py:387
  40.4 0.1 convert_reduce_fusion
  40.5 0.7 %concatenate.6.meta_ref = s32[15]{0:T(128)S(1)} concatenate(s32[1]{0:T(128)} %bitcast.1, s32[1]{0:T(128)} %bitcast.2, s32[6]{0:T(128)S(1)} %convert_reduce_fusion, s32[6]{0:T(128)S(1)} %get-tuple-element.25, s32[1]{0:T(128)} %bitcast.6), dimensions={0} | concatenate | bytes 120 | tf_op jit(solution)/shard_map/concatenate | solution.py:390
  41.2 0.0 collective-permute-done.10.refs_7_
  41.2 0.0 collective-permute-done.9.refs_5_
  41.2 0.0 collective-permute-done.8.refs_4_
  41.2 0.0 collective-permute-done.4.refs_2_
  41.2 1.8 %collective-permute-done.3.refs_1_ = f32[384,128]{1,0:T(8,128)S(1)} collective-permute-done((f32[384,128]{1,0:T(8,128)S(1)}, f32[384,128]{1,0:T(8,128)S(1)}, u32[]{:S(2)}, u32[]{:S(2)}) %collective-permute-start.3) | collective-permute-done | bytes 196640 | tf_op jit(solution)/shard_map/ppermute | solution.py:330
  43.0 6.4 %sign.14 = f32[768,128]{1,0:T(8,128)} custom-call(s32[15]{0:T(128)S(1)} %concatenate.6.meta_ref, f32[384,128]{1,0:T(8,128)S(1)} %add.63.refs_0_, f32[384,128]{1,0:T(8,128)S(1)} %collective-permute-done.3.refs_1_, f32[384,128]{1,0:T(8,128)S(1)} %collective-permute-done.4.refs_2_, f32[512,128]{1,0:T(8,128)S(1)} %add.65.refs_3_, ...), custom_call_target="tpu_custom_call" | custom-call | flops 3623878656 | bytes 2359296 | tf_op jit(solution)/shard_map/sign/pallas_call | solution.py:295
  (5 shorter events, 0.1 us)
Async XLA Ops:
  0.1 0.7 %copy-start = (f32[1,1,2048]{2,1,0:T(1,128)S(1)}, f32[1,1,2048]{2,1,0:T(1,128)}, u32[]{:S(2)}) copy-start(f32[1,1,2048]{2,1,0:T(1,128)} %potential_ref.3) | copy-start | bytes 24580
  8.3 31.4 %copy-start.1 = (s32[1,1,6]{2,1,0:T(1,128)S(1)}, s32[1,1,6]{2,1,0:T(1,128)}, u32[]{:S(2)}) copy-start(s32[1,1,6]{2,1,0:T(1,128)} %param.5) | copy-start | bytes 76
  8.3 8.2 %collective-permute-start.5 = (f32[256,128]{1,0:T(8,128)S(1)}, f32[256,128]{1,0:T(8,128)S(1)}, u32[]{:S(2)}, u32[]{:S(2)}) collective-permute-start(f32[256,128]{1,0:T(8,128)S(1)} %get-tuple-element.20), channel_id=1, source_target_pairs={{0,30},{2,4},{4,2},{6,8},{8,6},{10,12},{12,10},{14,16},{16,14},{18... | collective-permute-start | bytes 393224 | tf_op jit(solution)/shard_map/ppermute | solution.py:330
  13.8 2.7 %collective-permute-start.6 = (f32[256,128]{1,0:T(8,128)S(1)}, f32[256,128]{1,0:T(8,128)S(1)}, u32[]{:S(2)}, u32[]{:S(2)}) collective-permute-start(f32[256,128]{1,0:T(8,128)S(1)} %get-tuple-element.21), channel_id=1, source_target_pairs={{0,2},{2,0},{4,6},{6,4},{8,10},{10,8},{12,14},{14,12},{16,18},{18,... | collective-permute-start | bytes 393224 | tf_op jit(solution)/shard_map/ppermute | solution.py:330
  13.8 7.9 %collective-permute-start = (f32[384,128]{1,0:T(8,128)S(1)}, f32[384,128]{1,0:T(8,128)S(1)}, u32[]{:S(2)}, u32[]{:S(2)}) collective-permute-start(f32[384,128]{1,0:T(8,128)S(1)} %get-tuple-element.17), channel_id=1, source_target_pairs={{0,30},{2,4},{4,2},{6,8},{8,6},{10,12},{12,10},{14,16},{16,14},{18... | collective-permute-start | bytes 589832 | tf_op jit(solution)/shard_map/ppermute | solution.py:330
  14.6 7.1 %collective-permute-start.1 = (f32[384,128]{1,0:T(8,128)S(1)}, f32[384,128]{1,0:T(8,128)S(1)}, u32[]{:S(2)}, u32[]{:S(2)}) collective-permute-start(f32[384,128]{1,0:T(8,128)S(1)} %get-tuple-element.18), channel_id=1, source_target_pairs={{0,2},{2,0},{4,6},{6,4},{8,10},{10,8},{12,14},{14,12},{16,18},{18,... | collective-permute-start | bytes 589832 | tf_op jit(solution)/shard_map/ppermute | solution.py:330
  16.5 9.2 %collective-permute-start.7 = (f32[512,128]{1,0:T(8,128)S(1)}, f32[512,128]{1,0:T(8,128)S(1)}, u32[]{:S(2)}, u32[]{:S(2)}) collective-permute-start(f32[512,128]{1,0:T(8,128)S(1)} %maximum_add_fusion), channel_id=1, source_target_pairs={{0,1},{1,0},{2,3},{3,2},{4,5},{5,4},{6,7},{7,6},{8,9},{9,8},{10,11... | collective-permute-start | bytes 786440 | tf_op jit(solution)/shard_map/ppermute | solution.py:330
  18.5 22.6 %collective-permute-start.10 = (f32[512,128]{1,0:T(8,128)S(1)}, f32[512,128]{1,0:T(8,128)S(1)}, u32[]{:S(2)}, u32[]{:S(2)}) collective-permute-start(f32[512,128]{1,0:T(8,128)S(1)} %get-tuple-element.22.refs_6_), channel_id=1, source_target_pairs={{0,1},{1,0},{2,3},{3,2},{4,5},{5,4},{6,7},{7,6},{8,9},{9,8},{10,11... | collective-permute-start | bytes 786440 | tf_op jit(solution)/shard_map/ppermute | solution.py:330
  21.7 11.7 %collective-permute-start.2 = (f32[384,128]{1,0:T(8,128)S(1)}, f32[384,128]{1,0:T(8,128)S(1)}, u32[]{:S(2)}, u32[]{:S(2)}) collective-permute-start(f32[384,128]{1,0:T(8,128)S(1)} %add_add_fusion), channel_id=1, source_target_pairs={{0,1},{1,0},{2,3},{3,2},{4,5},{5,4},{6,7},{7,6},{8,9},{9,8},{10,11... | collective-permute-start | bytes 589832 | tf_op jit(solution)/shard_map/ppermute | solution.py:330
  25.8 15.4 %collective-permute-start.9 = (f32[256,128]{1,0:T(8,128)S(1)}, f32[256,128]{1,0:T(8,128)S(1)}, u32[]{:S(2)}, u32[]{:S(2)}) collective-permute-start(f32[256,128]{1,0:T(8,128)S(1)} %get-tuple-element.23), channel_id=1, source_target_pairs={{0,2},{2,0},{4,6},{6,4},{8,10},{10,8},{12,14},{14,12},{16,18},{18,... | collective-permute-start | bytes 393224 | tf_op jit(solution)/shard_map/ppermute | solution.py:330
  25.9 15.3 %collective-permute-start.8 = (f32[256,128]{1,0:T(8,128)S(1)}, f32[256,128]{1,0:T(8,128)S(1)}, u32[]{:S(2)}, u32[]{:S(2)}) collective-permute-start(f32[256,128]{1,0:T(8,128)S(1)} %get-tuple-element.24), channel_id=1, source_target_pairs={{0,30},{2,4},{4,2},{6,8},{8,6},{10,12},{12,10},{14,16},{16,14},{18... | collective-permute-start | bytes 393224 | tf_op jit(solution)/shard_map/ppermute | solution.py:330
  33.5 7.7 %collective-permute-start.4 = (f32[384,128]{1,0:T(8,128)S(1)}, f32[384,128]{1,0:T(8,128)S(1)}, u32[]{:S(2)}, u32[]{:S(2)}) collective-permute-start(f32[384,128]{1,0:T(8,128)S(1)} %add.63.refs_0_), channel_id=1, source_target_pairs={{0,2},{2,0},{4,6},{6,4},{8,10},{10,8},{12,14},{14,12},{16,18},{18,... | collective-permute-start | bytes 589832 | tf_op jit(solution)/shard_map/ppermute | solution.py:330
  33.5 9.5 %collective-permute-start.3 = (f32[384,128]{1,0:T(8,128)S(1)}, f32[384,128]{1,0:T(8,128)S(1)}, u32[]{:S(2)}, u32[]{:S(2)}) collective-permute-start(f32[384,128]{1,0:T(8,128)S(1)} %add.63.refs_0_), channel_id=1, source_target_pairs={{0,30},{2,4},{4,2},{6,8},{8,6},{10,12},{12,10},{14,16},{16,14},{18... | collective-permute-start | bytes 589832 | tf_op jit(solution)/shard_map/ppermute | solution.py:330
